TPU v7x, 256 devices: a whole 4x4x8 slice. The times are simulated.
256 devices in a mesh: row: 16 (over x, y), col: 16 (over z, core).
Axes of the slice: x: 4, y: 4, z: 8, core: 2. Of those that a mesh axis runs over, the one named last changes fastest.
Arguments:
- trailing_slab: float32 [131072, 2048], P('row', 'col'), may hold values from -6 to 6, as said below
- panel_columns: float32 [32, 131072], P(None, 'row'), may hold values from -1870.1934 to 1870.1934
- far_image: float32 [32, 131072], P(None, 'row'), may hold values from -2048 to 2048
Outputs:
- updated_slab: float32 [131072, 2048], P('row', 'col')
- update_factor: float32 [32, 131072], P(None, 'row')
Inputs may be any that keep to these rules, and one draw needn't show every extreme that they name: Rows 0 to 2047 of trailing_slab form a symmetric block.
All inputs are finite; a program needn't handle non-finite values.
Results may differ from a plain program's by a relative error of at most 0.0003.
Values sent between devices are 32-bit elements; how exact they have to be, the bound alone decides.
A program may use at most 64 MiB of HBM per device.

v0:
```python
import jax
import jax.numpy as jnp
from jax import lax
from jax.sharding import PartitionSpec as P


def from_root(block, axis, owner):
    block = jnp.where(lax.axis_index(axis) == owner, block, jnp.zeros_like(block))
    return lax.psum(block, axis)


def product(left, right):
    return jnp.dot(left, right, precision=lax.Precision.HIGHEST, preferred_element_type=jnp.float32)


def contract(left, right, left_dim, right_dim):
    return lax.dot_general(
        left,
        right,
        (((left_dim,), (right_dim,)), ((), ())),
        precision=lax.Precision.HIGHEST,
        preferred_element_type=jnp.float32,
    )


def cholesky_rows(gram_total):
    panel_width = gram_total.shape[0]
    identity = jnp.eye(panel_width, dtype=jnp.float32)
    indices = jnp.arange(panel_width)
    lower_part = jnp.zeros((panel_width, panel_width), jnp.float32)
    for column in range(panel_width):
        onehot = identity[column]
        residue = gram_total[:, column] - product(lower_part, lower_part[column])
        pivot = jnp.sqrt(jnp.sum(residue * onehot))
        new_column = jnp.where(indices >= column, residue / pivot, 0.0)
        lower_part = lower_part + new_column[:, None] * onehot[None, :]
    return lower_part


def invert_lower(lower_part):
    panel_width = lower_part.shape[0]
    identity = jnp.eye(panel_width, dtype=jnp.float32)
    inverse = jnp.zeros((panel_width, panel_width), jnp.float32)
    for index_row in range(panel_width):
        onehot = identity[index_row]
        pivot = jnp.sum(lower_part[index_row] * onehot)
        new_row = (onehot - product(lower_part[index_row], inverse)) / pivot
        inverse = inverse + onehot[:, None] * new_row[None, :]
    return inverse


def decompose(shifted):
    panel_width = shifted.shape[0]
    identity = jnp.eye(panel_width, dtype=jnp.float32)
    indices = jnp.arange(panel_width)
    lower_unit = identity
    upper_part = shifted
    for column in range(panel_width):
        factor = jnp.where(
            indices > column, upper_part[:, column] / upper_part[column, column], 0.0
        )
        lower_unit = lower_unit + factor[:, None] * identity[column][None, :]
        upper_part = upper_part - factor[:, None] * upper_part[column][None, :]
    return (lower_unit, jnp.triu(upper_part))


def factors(gram_total, top_rows):
    panel_width = gram_total.shape[0]
    identity = jnp.eye(panel_width, dtype=jnp.float32)
    cholesky_lower = cholesky_rows(gram_total)
    cholesky_inverse = invert_lower(cholesky_lower)
    top_factor = product(cholesky_inverse, top_rows).T
    sign_flip = jnp.where(jnp.diag(top_factor) >= 0.0, -1.0, 1.0).astype(jnp.float32)
    lower_unit, upper_part = decompose(identity - top_factor * sign_flip[None, :])
    upper_inverse = invert_lower(upper_part.T).T
    root_inverse = cholesky_inverse.T
    mixing = -product(root_inverse * sign_flip[None, :], upper_inverse)
    lower_inverse = invert_lower(lower_unit)
    triangle = product(upper_part, lower_inverse.T)
    return (mixing, upper_inverse, triangle)


def local(trailing_slab, panel_columns, far_image):
    cols_dev = trailing_slab.shape[1]
    panel_width = panel_columns.shape[0]
    row_pos = lax.axis_index("row")
    col_pos = lax.axis_index("col")
    top_row = row_pos == 0
    gram_part = product(panel_columns, panel_columns.T)
    top_local = panel_columns[:, :panel_width]
    gram_total = lax.psum(gram_part, "row")
    top_rows = from_root(top_local, "row", 0)
    mixing, upper_inverse, triangle = factors(gram_total, top_rows)
    reflectors = product(mixing.T, panel_columns)
    head_rows = jnp.where(top_row, upper_inverse.T, 0.0)
    reflectors = reflectors.at[:, :panel_width].add(head_rows)
    col_start = col_pos * cols_dev
    own_reflectors = from_root(
        lax.dynamic_slice_in_dim(reflectors, col_start, cols_dev, 1), "row", 0
    )
    far_part = product(mixing.T, far_image)
    local_image = contract(own_reflectors, trailing_slab, 1, 1)
    images = lax.psum(local_image, "col") + far_part
    inner_block = lax.psum(product(reflectors, images.T), "row")
    core_block = product(product(triangle.T, inner_block), triangle)
    weights = product(triangle.T, images) - 0.5 * product(core_block.T, reflectors)
    own_weights = from_root(lax.dynamic_slice_in_dim(weights, col_start, cols_dev, 1), "row", 0)
    updated = (
        trailing_slab
        - contract(reflectors, own_weights, 0, 0)
        - contract(weights, own_reflectors, 0, 0)
    )
    return (updated, weights)


def solution(mesh):
    in_specs = (P("row", "col"), P(None, "row"), P(None, "row"))
    out_specs = (P("row", "col"), P(None, "row"))
    return jax.shard_map(local, mesh=mesh, in_specs=in_specs, out_specs=out_specs, check_vma=False)
```

profile of v0, /device:TPU:0, one launch (start us, length us, event | category | flops | bytes accessed | tf_op | source)
XLA Modules:
  0.0 674.7 jit_solution(5860183124567604668)
XLA Ops:
  9.0 2.5 fusion.969
  12.3 72.9 %all-reduce = (f32[32,32]{0,1:T(8,128)S(1)}, f32[32,32]{1,0:T(8,128)S(1)}) all-reduce(f32[32,32]{0,1:T(8,128)S(1)} %broadcast_select_fusion, f32[32,32]{1,0:T(8,128)S(1)} %fusion.969), channel_id=1, replica_groups=mesh['row'=16,'col'=16] {'row'}, use_global_device_ids=true, to_apply=%region_65.66 | all-reduce | flops 2048 | bytes 16384 | tf_op jit(solution)/shard_map/psum | solution.py:9
  166.8 0.9 fusion.131
  171.0 0.9 fusion.136
  171.9 0.9 fusion.137
  172.8 0.9 fusion.138
  174.5 0.9 fusion.140
  181.4 0.9 fusion.148
  183.2 0.9 fusion.150
  191.8 0.9 fusion.160
  250.5 0.9 fusion.195
  252.9 0.9 fusion.197
  255.3 0.9 fusion.199
  257.7 0.9 fusion.201
  260.0 0.9 fusion.203
  267.6 0.9 fusion.168
  268.5 0.9 fusion.169
  269.4 1.0 fusion.170
  270.4 0.9 fusion.171
  271.3 0.9 fusion.172
  273.7 0.9 fusion.206
  276.1 0.9 fusion.208
  279.3 0.9 fusion.176
  281.8 0.9 fusion.178
  285.7 0.9 fusion.210
  287.5 0.9 fusion.212
  289.9 0.9 fusion.182
  293.8 0.9 fusion.214
  295.5 0.9 fusion.216
  297.9 0.9 fusion.186
  301.8 0.9 fusion.218
  303.5 0.9 fusion.220
  306.0 0.9 fusion.190
  308.3 0.9 fusion.192
  309.6 1.3 fusion.970
  312.1 69.5 %psum.44 = f32[32,128]{1,0:T(8,128)S(1)} all-reduce(f32[32,128]{1,0:T(8,128)S(1)} %dynamic-slice_select_fusion.1), channel_id=1, replica_groups=mesh['row'=16,'col'=16] {'row'}, use_global_device_ids=true, to_apply=%region_131.132 | all-reduce | flops 4096 | bytes 32768 | tf_op jit(solution)/shard_map/psum | solution.py:9
  381.6 7.4 %fusion.971 = f32[32,8192]{1,0:T(8,128)} fusion(f32[32,128]{1,0:T(8,128)S(1)} %psum.44, f32[8192,128]{1,0:T(8,128)} %param.5), kind=kOutput, calls=%fused_computation.1690 | convolution fusion | flops 402653184 | bytes 5259264 | tf_op jit(solution)/shard_map/dot_general | solution.py:17
  389.7 0.9 fusion.222
  391.5 0.9 fusion.224
  392.6 106.0 %all-reduce.3.cloned.1.call-done = f32[32,8192]{1,0:T(8,128)} async-done(((f32[32,8192]{1,0:T(8,128)}), f32[32,8192]{1,0:T(8,128)}) %all-reduce.3.cloned.1.call-update) | async-done | bytes 1048592 | tf_op jit(solution)/shard_map/psum | solution.py:103
  498.6 2.3 convolution_add_fusion
  500.9 1.0 fusion.973
  501.8 2.0 fusion.972
  503.9 74.2 %psum.46 = f32[32,32]{1,0:T(8,128)S(1)} all-reduce(f32[32,32]{1,0:T(8,128)S(1)} %fusion.973), channel_id=1, replica_groups=mesh['row'=16,'col'=16] {'row'}, use_global_device_ids=true, to_apply=%region_133.134 | all-reduce | flops 1024 | bytes 8192 | tf_op jit(solution)/shard_map/psum | solution.py:104
  578.5 2.3 fusion
  580.8 69.8 %psum.47 = f32[32,128]{1,0:T(8,128)S(1)} all-reduce(f32[32,128]{1,0:T(8,128)S(1)} %dynamic-slice_select_fusion), channel_id=1, replica_groups=mesh['row'=16,'col'=16] {'row'}, use_global_device_ids=true, to_apply=%region_134.135 | all-reduce | flops 4096 | bytes 32768 | tf_op jit(solution)/shard_map/psum | solution.py:9
  650.6 8.5 %convolution_subtract_fusion.1 = f32[8192,128]{1,0:T(8,128)S(1)} fusion(f32[8192,128]{1,0:T(8,128)} %param.5, f32[32,8192]{1,0:T(8,128)S(1)} %scatter-add.4, f32[32,128]{1,0:T(8,128)S(1)} %psum.47), kind=kOutput, calls=%fused_computation.2 | convolution fusion | flops 403701760 | bytes 9453568 | tf_op jit(solution)/shard_map/dot_general | solution.py:17
  659.1 8.3 %convolution_subtract_fusion = f32[8192,128]{1,0:T(8,128)} fusion(f32[8192,128]{1,0:T(8,128)S(1)} %convolution_subtract_fusion.1, f32[32,8192]{1,0:T(8,128)S(1)} %fusion, f32[32,128]{1,0:T(8,128)S(1)} %psum.44), kind=kOutput, calls=%fused_computation.1 | convolution fusion | flops 403701760 | bytes 9453568 | tf_op jit(solution)/shard_map/dot_general | solution.py:17
  (419 shorter events, 178.7 us)
Async XLA Ops:
  7.2 491.5 %copy-start = (f32[32,8192]{1,0:T(8,128)S(1)}, f32[32,8192]{1,0:T(8,128)}, u32[]{:S(2)}) copy-start(f32[32,8192]{1,0:T(8,128)} %param.7) | copy-start | bytes 3145732
  7.2 491.4 %all-reduce.3.cloned.1.call-start = ((), (), s32[]{:S(2)}) async-start(), calls=%async_computation | async-start | bytes 2097152 | tf_op jit(solution)/shard_map/psum | solution.py:103
  269.4 40.2 %copy-start.1 = (f32[32,8192]{1,0:T(8,128)S(1)}, f32[32,8192]{1,0:T(8,128)}, u32[]{:S(2)}) copy-start(f32[32,8192]{1,0:T(8,128)} %param.6) | copy-start | bytes 3145732
  580.8 78.4 %copy-start.2 = (f32[32,8192]{1,0:T(8,128)}, f32[32,8192]{1,0:T(8,128)S(1)}, u32[]{:S(2)}) copy-start(f32[32,8192]{1,0:T(8,128)S(1)} %fusion) | copy-start | bytes 3145732
Sparse Core Ops, SparseCore 0:
  389.1 109.4 all-reduce.2
where the time goes:
time: 686 us; the launch traced here: 675 us
  blocking collectives  286 us (42%)
  matrix products  141 us (21%)
  waiting for transfers between devices  106 us (15%)
  other arithmetic  66 us (10%)
  between operations  37.9 us (6%)
  local copies, waits for them, and re-layouts  36.8 us (5%)
    psum x3, blocking collectives, from_root(): return lax.psum(block, axis)  212 us
    dot_general x139, matrix products, product(): jnp.dot(left, right, precision=lax.Precision.HIGHEST, preferred_element_t...  117 us
    psum x1, waiting for transfers between devices, local(): images = lax.psum(local_image, 'col') + far_part  106 us
    psum x1, blocking collectives, local(): inner_block = lax.psum(product(reflectors, images.T), 'row')  74.2 us
    reduce_sum x49, other arithmetic, invert_lower(): pivot = jnp.sum(lower_part[index_row] * onehot)  31.5 us
    dot_general x3, matrix products, contract(): lax.dot_general(left, right, (((left_dim,), (right_dim,)), ((), ())), pre...  24.2 us
    mul x32, other arithmetic, decompose(): upper_part = upper_part - factor[:, None] * upper_part[column][None, :]  21 us
    slice x32, local copies, waits for them, and re-layouts, decompose(): upper_part[column, column]  18.6 us
  transfers between devices with their start and end apart: 1, of which 1 were waited for; matrix products, arithmetic and copies ran while one was open for 1% of the time, Pallas kernels for 0%

commit v1 on v0

v1 whole, which is shorter than its diff:
```python
import functools

import jax
import jax.numpy as jnp
from jax import lax
from jax.experimental import pallas as pl
from jax.experimental.pallas import tpu as pltpu
from jax.sharding import PartitionSpec as P

F32 = jnp.float32
BF16 = jnp.bfloat16
MESH = pl.DeviceIdType.MESH
NT = (((1,), (1,)), ((), ()))
TN = (((0,), (0,)), ((), ()))
NN = (((1,), (0,)), ((), ()))


def exact(left, right, dims=NN):
    return lax.dot_general(
        left, right, dims, precision=lax.Precision.HIGHEST, preferred_element_type=F32
    )


def narrow(left, right, dims):
    return lax.dot_general(left, right, dims, preferred_element_type=F32)


def split(x):
    high = x.astype(BF16)
    low = (x - high.astype(F32)).astype(BF16)
    return high, low


def split3(x):
    high = x.astype(BF16)
    rest = x - high.astype(F32)
    mid = rest.astype(BF16)
    low = (rest - mid.astype(F32)).astype(BF16)
    return high, mid, low


def gram_of(block):
    nb = block.shape[0]
    one, two, three = split3(block)
    first = narrow(jnp.concatenate([one, two, three], 0), one, NT)
    second = narrow(jnp.concatenate([one, two], 0), two, NT)
    third = narrow(one, three, NT)
    return (
        first[:nb]
        + (first[nb : 2 * nb] + second[:nb])
        + (first[2 * nb :] + second[nb:] + third)
    )


def cross(left, right):
    nb = left.shape[0]
    lh, ll = split(left)
    rh, rl = split(right)
    both = narrow(jnp.concatenate([lh, ll], 0), rh, NT)
    return both[:nb] + both[nb:] + narrow(lh, rl, NT)


def eliminate(tables, nb):
    rows = lax.broadcasted_iota(jnp.int32, (nb, 128), 0)
    for j in range(nb):
        done = []
        for table in tables:
            column = jnp.broadcast_to(table[:, j : j + 1], (nb, 128))
            pivot_row = table[j : j + 1, :] / column[j : j + 1, :]
            done.append(table - jnp.where(rows > j, column, 0.0) * pivot_row)
        tables = done
    return tables


def pack(square):
    total = square[0:8]
    for k in range(1, 4):
        total = total + pltpu.roll(square[8 * k : 8 * k + 8], 32 * k, 1)
    return total


def unpack(packed, lanes):
    parts = [packed] + [pltpu.roll(packed, 128 - 32 * k, 1) for k in range(1, 4)]
    return jnp.where(lanes < 32, jnp.concatenate(parts, 0), 0.0)


def wide(square):
    return jnp.concatenate([square, jnp.zeros((square.shape[0], 128 - square.shape[1]), F32)], 1)


def exchange_kernel(
    nrow, ncol,
    slab, panel, far,
    images, coefs,
    pv, sv, fv, gsend, gbuf, headbuf, topbuf, pt, zout, pbuf, zsum, rbuf, zown,
    osend, obuf, h1send, h1buf, h2send, h2buf,
    load_sem, g_ssem, g_rsem, t_ssem, t_rsem, p_ssem, p_rsem, r_ssem, r_rsem,
    a_ssem, a_rsem, f_ssem, o_ssem, o_rsem, h1_ssem, h1_rsem, h2_ssem, h2_rsem,
    image_sem,
):
    nb = 32
    nz = ncol // 2
    chunk = pv.shape[1] // ncol
    row = lax.axis_index("row")
    col = lax.axis_index("col")
    z = lax.div(col, 2)
    core = lax.rem(col, 2)
    partner = col + 1 - 2 * core
    rows = lax.broadcasted_iota(jnp.int32, (nb, 128), 0)
    lanes = lax.broadcasted_iota(jnp.int32, (nb, 128), 1)

    def remote(src, dst, ssem, rsem, device):
        return pltpu.make_async_remote_copy(
            src_ref=src, dst_ref=dst, send_sem=ssem, recv_sem=rsem,
            device_id=device, device_id_type=MESH,
        )

    def row_peer(k):
        return lax.rem(row + k, nrow)

    def col_peer(k):
        return lax.rem(col + k, ncol)

    def z_peer(k):
        return lax.rem(z + k, nz)

    load_p = pltpu.make_async_copy(panel, pv, load_sem.at[0])
    load_s = pltpu.make_async_copy(slab, sv, load_sem.at[1])
    own = core * nz + z
    own_columns = pl.ds(pl.multiple_of(own * chunk, chunk), chunk)
    load_f = pltpu.make_async_copy(far.at[:, own_columns], fv, load_sem.at[2])
    load_p.start()
    load_s.start()
    load_f.start()

    barrier = pltpu.get_barrier_semaphore()

    @pl.loop(1, nrow)
    def _(k):
        pl.semaphore_signal(barrier, inc=1, device_id={"row": row_peer(k)}, device_id_type=MESH)

    @pl.loop(1, ncol)
    def _(k):
        pl.semaphore_signal(barrier, inc=1, device_id={"col": col_peer(k)}, device_id_type=MESH)

    load_p.wait()
    gram = jnp.zeros((nb, nb), F32)
    for g in range(ncol):
        gram = gram + gram_of(pv[:, g * chunk : (g + 1) * chunk])
    gsend[...] = pack(wide(gram))
    gbuf[row] = gsend[...]
    pl.semaphore_wait(barrier, nrow + ncol - 2)

    head_columns = pl.ds(pl.multiple_of(col * 128, 128), 128)

    @pl.when(row == 0)
    def _():
        local_head = pltpu.make_async_copy(pv.at[:, head_columns], headbuf, load_sem.at[3])
        local_top = pltpu.make_async_copy(pv.at[:, pl.ds(0, 128)], topbuf, load_sem.at[4])
        local_head.start()
        local_top.start()

        @pl.loop(1, nrow)
        def _(k):
            peer = row_peer(k)
            remote(topbuf_src(pv), topbuf, t_ssem.at[0, k], t_rsem.at[0], {"row": peer}).start()
            remote(pv.at[:, head_columns], headbuf, t_ssem.at[1, k], t_rsem.at[1], {"row": peer}).start()

        local_head.wait()
        local_top.wait()

    @pl.loop(1, nrow)
    def _(k):
        remote(gsend, gbuf.at[row], g_ssem.at[k], g_rsem.at[row], {"row": row_peer(k)}).start()

    @pl.when(row != 0)
    def _():
        remote(topbuf_src(pv), topbuf, t_ssem.at[0, 0], t_rsem.at[0], {"row": 0}).wait_recv()
        remote(pv.at[:, head_columns], headbuf, t_ssem.at[1, 0], t_rsem.at[1], {"row": 0}).wait_recv()

    @pl.loop(1, nrow)
    def _(k):
        peer = row_peer(k)
        remote(gsend, gbuf.at[peer], g_ssem.at[k], g_rsem.at[peer], {"row": peer}).wait_recv()

    total = gbuf[0]
    for r in range(1, nrow):
        total = total + gbuf[r]
    table = (
        unpack(total, lanes)
        + jnp.where(lanes == rows + nb, 1.0, 0.0)
        + pltpu.roll(jnp.where(lanes < nb, topbuf[...], 0.0), 2 * nb, 1)
    )
    (table,) = eliminate([table], nb)
    pivots = jnp.sum(jnp.where(lanes == rows, table, 0.0), axis=1, keepdims=True)
    table = table / jnp.sqrt(pivots)
    signs = jnp.sum(jnp.where(lanes == rows + 2 * nb, table, 0.0), axis=1, keepdims=True)
    flip = jnp.where(signs >= 0.0, -1.0, 1.0).astype(F32)
    upper = jnp.where((lanes >= rows) & (lanes < nb), table * flip, 0.0)
    unit = jnp.where(lanes == rows, 1.0, 0.0)[:, :nb]
    correction = wide(exact(upper[:, :nb], unit, TN))
    flipped_inverse = (pltpu.roll(table, 128 - nb, 1) * flip)[:, :nb]
    shifted_t = jnp.where(lanes == rows, 1.0, 0.0) - jnp.where(
        lanes < nb, pltpu.roll(table, 128 - 2 * nb, 1) * flip, 0.0
    )

    @pl.when(col == 0)
    def _():
        headbuf[...] = headbuf[...] - correction

    pt[...] = pv[...]

    @pl.when(row == 0)
    def _():
        pt[:, 0:128] = pt[:, 0:128] - correction

    load_s.wait()
    high, low = split(headbuf[...])
    weights = jnp.concatenate(
        [
            jnp.concatenate([high, high], 1),
            jnp.concatenate([low, jnp.zeros_like(low)], 1),
        ],
        0,
    )

    def image_chunk(index):
        block = sv[pl.ds(pl.multiple_of(index * chunk, chunk), chunk), :]
        sh, sl = split(block)
        both = narrow(weights, jnp.concatenate([sh, sl], 1), NT)
        return both[:nb] + both[nb:]

    @pl.loop(1, nz + 1)
    def _(k):
        peer = z_peer(k)
        zout[peer] = image_chunk((1 - core) * nz + peer)

    @pl.loop(1, nz + 1)
    def _(k):
        peer = z_peer(k)
        remote(zout.at[peer], pbuf.at[peer], p_ssem.at[peer], p_rsem.at[peer], {"col": partner}).start()

    @pl.loop(1, nz + 1)
    def _(k):
        peer = z_peer(k)
        part = image_chunk(core * nz + peer)
        remote(zout.at[peer], pbuf.at[peer], p_ssem.at[peer], p_rsem.at[peer], {"col": partner}).wait_recv()
        zsum[peer] = part + pbuf[peer]

    @pl.loop(1, nz)
    def _(k):
        peer = z_peer(k)
        remote(zsum.at[peer], rbuf.at[z], r_ssem.at[peer], r_rsem.at[z], {"col": 2 * peer + core}).start()

    load_f.wait()

    @pl.when(row == 0)
    def _():
        head = sv.shape[1] * ncol
        ph, plow = split(pt[:, 0:head])
        sh, sl = split(sv[0:head, :])
        both = narrow(jnp.concatenate([ph, plow], 0), sh, NN)
        osend[...] = both[:nb] + both[nb:] + narrow(ph, sl, NN)

    @pl.when(row == 0)
    def _():
        extra = pltpu.make_async_copy(far.at[:, head_columns], obuf, load_sem.at[5])
        extra.start()
        extra.wait()
        osend[...] = osend[...] + obuf[...]
        obuf[...] = osend[...]

        @pl.loop(1, nrow)
        def _(k):
            remote(osend, obuf, o_ssem.at[k], o_rsem, {"row": row_peer(k)}).start()

    inner = cross(fv[...], pt[:, own_columns])
    for g in range(nz):
        columns = pl.ds(pl.multiple_of((core * nz + g) * chunk, chunk), chunk)
        inner = inner + cross(zsum[g], pt[:, columns])
    h1send[...] = pack(wide(inner))
    h1buf[row] = h1send[...]

    @pl.loop(1, nrow)
    def _(k):
        remote(h1send, h1buf.at[row], h1_ssem.at[k], h1_rsem.at[row], {"row": row_peer(k)}).start()

    shifted = wide(exact(shifted_t[:, :nb], unit, TN))
    augment = jnp.where(lanes == rows + nb, 1.0, 0.0)
    lower_table, upper_table = eliminate([shifted + augment, shifted_t + augment], nb)
    diagonal = jnp.sum(jnp.where(lanes == rows, upper_table, 0.0), axis=1, keepdims=True)
    lower_inverse = pltpu.roll(lower_table, 128 - nb, 1)[:, :nb]
    upper_inverse_t = (pltpu.roll(upper_table, 128 - nb, 1) / diagonal)[:, :nb]
    mixing_t = -exact(upper_inverse_t, flipped_inverse)
    second_t = -exact(lower_inverse, flipped_inverse)
    kernel_t = exact(second_t, mixing_t, TN)
    own_reflectors = exact(mixing_t, headbuf[...])
    bottom = exact(second_t, own_reflectors, TN)

    @pl.loop(1, nrow)
    def _(k):
        peer = row_peer(k)
        remote(h1send, h1buf.at[peer], h1_ssem.at[k], h1_rsem.at[peer], {"row": peer}).wait_recv()

    share = h1buf[0]
    for r in range(1, nrow):
        share = share + h1buf[r]
    h2send[...] = share
    h2buf[col] = share

    @pl.loop(1, nz)
    def _(k):
        peer = z_peer(k)
        remote(zsum.at[peer], rbuf.at[peer], r_ssem.at[peer], r_rsem.at[peer], {"col": 2 * peer + core}).wait_recv()

    rbuf[z] = zsum[z]
    chunk_sum = fv[...]
    for r in range(nz):
        chunk_sum = chunk_sum + rbuf[r]
    zown[...] = chunk_sum

    @pl.loop(1, ncol)
    def _(k):
        remote(h2send, h2buf.at[col], h2_ssem.at[k], h2_rsem.at[col], {"col": col_peer(k)}).start()

    keep = pltpu.make_async_copy(zown, images.at[own], image_sem)
    keep.start()
    remote(zown, images.at[own], f_ssem.at[z], a_rsem.at[own], {"col": partner}).start()

    @pl.loop(1, nz)
    def _(k):
        peer = z_peer(k)
        remote(zown, images.at[own], a_ssem.at[peer], a_rsem.at[own], {"col": 2 * peer + core}).start()

    @pl.when(row != 0)
    def _():
        remote(osend, obuf, o_ssem.at[0], o_rsem, {"row": 0}).wait_recv()

    @pl.loop(1, ncol)
    def _(k):
        peer = col_peer(k)
        remote(h2send, h2buf.at[peer], h2_ssem.at[k], h2_rsem.at[peer], {"col": peer}).wait_recv()

    inner_total = h2buf[0]
    for c in range(1, ncol):
        inner_total = inner_total + h2buf[c]
    inner_t = unpack(inner_total, lanes)[:, :nb]
    weight_t = -0.5 * exact(exact(second_t, inner_t), kernel_t)
    own_weights = exact(second_t, obuf[...]) + exact(weight_t, headbuf[...])
    top_part = exact(mixing_t, own_weights, TN) + exact(weight_t, own_reflectors, TN)
    coefs[0:nb, :] = top_part
    coefs[nb : 2 * nb, :] = bottom
    coefs[2 * nb : 3 * nb, :] = wide(jnp.concatenate([weight_t, second_t], 1))
    coefs[3 * nb :, :] = jnp.where(row == 0, correction, 0.0)

    def gathered(index, ssem):
        slot = images.at[index]
        return remote(slot, slot, ssem, a_rsem.at[index], {"col": partner})

    @pl.loop(1, nz)
    def _(k):
        peer = z_peer(k)
        copy = gathered(core * nz + peer, f_ssem.at[peer])
        copy.wait_recv()
        copy.start()

    @pl.loop(0, nz)
    def _(k):
        peer = z_peer(k)
        gathered((1 - core) * nz + peer, f_ssem.at[peer]).wait_recv()

    keep.wait()

    @pl.loop(0, nz)
    def _(k):
        remote(zout.at[k], pbuf.at[k], p_ssem.at[k], p_rsem.at[k], {"col": partner}).wait_send()
        gathered(core * nz + k, f_ssem.at[k]).wait_send()

    @pl.loop(1, nz)
    def _(k):
        peer = z_peer(k)
        device = {"col": 2 * peer + core}
        remote(zsum.at[peer], rbuf.at[z], r_ssem.at[peer], r_rsem.at[z], device).wait_send()
        remote(zown, images.at[own], a_ssem.at[peer], a_rsem.at[own], device).wait_send()

    @pl.loop(1, nrow)
    def _(k):
        device = {"row": row_peer(k)}
        remote(gsend, gbuf.at[row], g_ssem.at[k], g_rsem.at[row], device).wait_send()
        remote(h1send, h1buf.at[row], h1_ssem.at[k], h1_rsem.at[row], device).wait_send()

    @pl.loop(1, ncol)
    def _(k):
        remote(h2send, h2buf.at[col], h2_ssem.at[k], h2_rsem.at[col], {"col": col_peer(k)}).wait_send()

    @pl.when(row == 0)
    def _():
        @pl.loop(1, nrow)
        def _(k):
            device = {"row": row_peer(k)}
            remote(topbuf_src(pv), topbuf, t_ssem.at[0, k], t_rsem.at[0], device).wait_send()
            remote(pv.at[:, head_columns], headbuf, t_ssem.at[1, k], t_rsem.at[1], device).wait_send()
            remote(osend, obuf, o_ssem.at[k], o_rsem, device).wait_send()


def topbuf_src(pv):
    return pv.at[:, pl.ds(0, 128)]


def update_kernel(slab, panel, images, coefs, updated, factor, xs):
    nb = 32
    parts = images.shape[0]
    chunk = images.shape[2]
    first = pl.program_id(0) == 0
    bh, bl = split(coefs[0 : 2 * nb, :])
    right = jnp.concatenate([bh, bl, bh], 0)
    ch, cl = split(coefs[2 * nb : 3 * nb, 0 : 2 * nb])
    left = jnp.concatenate([ch, ch, cl], 1)
    xs[:nb, :] = panel[...]

    @pl.when(first)
    def _():
        xs[:nb, 0:128] = xs[:nb, 0:128] - coefs[3 * nb :, :]

    for g in range(parts):
        xs[nb:, g * chunk : (g + 1) * chunk] = images[g]
    for g in range(parts):
        piece = slice(g * chunk, (g + 1) * chunk)
        xh, xl = split(xs[:, piece])
        factor[:, piece] = narrow(left, jnp.concatenate([xh, xl, xh], 0), NN)
        stacked = jnp.concatenate([xh, xh, xl], 0)
        updated[piece, :] = slab[piece, :] - narrow(stacked, right, TN)


def local(nrow, ncol, slab, panel, far):
    nb, length = panel.shape
    chunk = length // ncol
    nz = ncol // 2
    anywhere = pl.BlockSpec(memory_space=pl.ANY)
    vmem = pl.BlockSpec(memory_space=pltpu.VMEM)
    dma = pltpu.SemaphoreType.DMA
    images, coefs = pl.pallas_call(
        functools.partial(exchange_kernel, nrow, ncol),
        name="exchange",
        out_shape=(
            jax.ShapeDtypeStruct((ncol, nb, chunk), F32),
            jax.ShapeDtypeStruct((4 * nb, 128), F32),
        ),
        in_specs=[anywhere] * 3,
        out_specs=(anywhere, vmem),
        scratch_shapes=[
            pltpu.VMEM((nb, length), F32),
            pltpu.VMEM(slab.shape, F32),
            pltpu.VMEM((nb, chunk), F32),
            pltpu.VMEM((8, 128), F32),
            pltpu.VMEM((nrow, 8, 128), F32),
            pltpu.VMEM((nb, 128), F32),
            pltpu.VMEM((nb, 128), F32),
            pltpu.VMEM((nb, length), F32),
            pltpu.VMEM((nz, nb, chunk), F32),
            pltpu.VMEM((nz, nb, chunk), F32),
            pltpu.VMEM((nz, nb, chunk), F32),
            pltpu.VMEM((nz, nb, chunk), F32),
            pltpu.VMEM((nb, chunk), F32),
            pltpu.VMEM((nb, 128), F32),
            pltpu.VMEM((nb, 128), F32),
            pltpu.VMEM((8, 128), F32),
            pltpu.VMEM((nrow, 8, 128), F32),
            pltpu.VMEM((8, 128), F32),
            pltpu.VMEM((ncol, 8, 128), F32),
            dma((6,)),
            dma((nrow,)), dma((nrow,)),
            dma((2, nrow)), dma((2,)),
            dma((nz,)), dma((nz,)),
            dma((nz,)), dma((nz,)),
            dma((nz,)), dma((ncol,)), dma((nz,)),
            dma((nrow,)), dma(()),
            dma((nrow,)), dma((nrow,)),
            dma((ncol,)), dma((ncol,)),
            dma(()),
        ],
        compiler_params=pltpu.CompilerParams(
            collective_id=0, has_side_effects=True, vmem_limit_bytes=32 * 2**20
        ),
    )(slab, panel, far)
    steps = 4
    wide_rows = length // steps
    parts = ncol // steps
    return pl.pallas_call(
        update_kernel,
        name="update",
        grid=(steps,),
        out_shape=(
            jax.ShapeDtypeStruct(slab.shape, F32),
            jax.ShapeDtypeStruct(panel.shape, F32),
        ),
        in_specs=[
            pl.BlockSpec((wide_rows, 128), lambda i: (i, 0)),
            pl.BlockSpec((nb, wide_rows), lambda i: (0, i)),
            pl.BlockSpec((parts, nb, chunk), lambda i: (i, 0, 0)),
            pl.BlockSpec((4 * nb, 128), lambda i: (0, 0)),
        ],
        out_specs=(
            pl.BlockSpec((wide_rows, 128), lambda i: (i, 0)),
            pl.BlockSpec((nb, wide_rows), lambda i: (0, i)),
        ),
        scratch_shapes=[pltpu.VMEM((2 * nb, wide_rows), F32)],
        compiler_params=pltpu.CompilerParams(vmem_limit_bytes=32 * 2**20),
    )(slab, panel, images, coefs)


def solution(mesh):
    sizes = dict(mesh.shape)
    body = functools.partial(local, sizes["row"], sizes["col"])
    in_specs = (P("row", "col"), P(None, "row"), P(None, "row"))
    out_specs = (P("row", "col"), P(None, "row"))
    return jax.shard_map(body, mesh=mesh, in_specs=in_specs, out_specs=out_specs, check_vma=False)
```

time: 686 us -> 66.5 us (0.10)
  the two profiles are of different devices: /device:TPU:0 before, /device:TPU:37 now
where the time goes in v1:
time: 66.5 us; the launch traced here: 66.3 us
  Pallas kernels  61 us (92%)
  local copies, waits for them, and re-layouts  4.63 us (7%)
    pallas_call x1, Pallas kernels, local(): pl.pallas_call(functools.partial(exchange_kernel, nrow, ncol), name='exch...  57 us
    unnamed x6, local copies, waits for them, and re-layouts  4.63 us
    pallas_call x1, Pallas kernels, local(): pl.pallas_call(update_kernel, name='update', grid=(steps,), out_shape=(ja...  4.06 us

profile of v1, /device:TPU:37, one launch (start us, length us, event | category | flops | bytes accessed | tf_op | source)
XLA Modules:
  0.0 66.3 jit_solution(12139842342615253930)
XLA Ops:
  0.6 0.0 copy-start
  0.6 2.2 %copy-done = f32[8192,128]{1,0:T(8,128)S(1)} copy-done((f32[8192,128]{1,0:T(8,128)S(1)}, f32[8192,128]{1,0:T(8,128)}, u32[]{:S(2)}) %copy-start) | copy-done | bytes 4194328
  2.8 0.0 copy-start.1
  2.8 1.2 %copy-done.1 = f32[32,8192]{1,0:T(8,128)S(1)} copy-done((f32[32,8192]{1,0:T(8,128)S(1)}, f32[32,8192]{1,0:T(8,128)}, u32[]{:S(2)}) %copy-start.1) | copy-done | bytes 1048600
  4.0 0.0 copy-start.2
  4.0 1.2 %copy-done.2 = f32[32,8192]{1,0:T(8,128)S(1)} copy-done((f32[32,8192]{1,0:T(8,128)S(1)}, f32[32,8192]{1,0:T(8,128)}, u32[]{:S(2)}) %copy-start.2) | copy-done | bytes 1048600
  5.3 57.0 %exchange.1 = (f32[16,32,512]{2,1,0:T(8,128)S(1)}, f32[128,128]{1,0:T(8,128)S(1)}) custom-call(f32[8192,128]{1,0:T(8,128)S(1)} %copy-done, f32[32,8192]{1,0:T(8,128)S(1)} %copy-done.1, f32[32,8192]{1,0:T(8,128)S(1)} %copy-done.2), custom_call_target="tpu_custom_call" | custom-call | tf_op jit(solution)/shard_map/exchange/pallas_call | solution.py:442
  62.2 4.1 %update.1 = (f32[8192,128]{1,0:T(8,128)}, f32[32,8192]{1,0:T(8,128)}) custom-call(f32[8192,128]{1,0:T(8,128)S(1)} %copy-done, f32[32,8192]{1,0:T(8,128)S(1)} %copy-done.1, f32[16,32,512]{2,1,0:T(8,128)S(1)} %get-tuple-element.4.images, f32[128,128]{1,0:T(8,128)S(1)} %get-tuple-element.5.coefs), custom_call_target="tpu_custom_call" | custom-call | tf_op jit(solution)/shard_map/update/pallas_call | solution.py:489
Async XLA Ops:
  0.6 2.2 %copy-start = (f32[8192,128]{1,0:T(8,128)S(1)}, f32[8192,128]{1,0:T(8,128)}, u32[]{:S(2)}) copy-start(f32[8192,128]{1,0:T(8,128)} %slab.3) | copy-start | bytes 12582916
  2.8 1.2 %copy-start.1 = (f32[32,8192]{1,0:T(8,128)S(1)}, f32[32,8192]{1,0:T(8,128)}, u32[]{:S(2)}) copy-start(f32[32,8192]{1,0:T(8,128)} %panel.3) | copy-start | bytes 3145732
  4.0 1.2 %copy-start.2 = (f32[32,8192]{1,0:T(8,128)S(1)}, f32[32,8192]{1,0:T(8,128)}, u32[]{:S(2)}) copy-start(f32[32,8192]{1,0:T(8,128)} %far.1) | copy-start | bytes 3145732

commit v2 on v1

v2 whole, which is shorter than its diff:
```python
import functools

import jax
import jax.numpy as jnp
from jax import lax
from jax.experimental import pallas as pl
from jax.experimental.pallas import tpu as pltpu
from jax.sharding import PartitionSpec as P

F32 = jnp.float32
BF16 = jnp.bfloat16
MESH = pl.DeviceIdType.MESH
NT = (((1,), (1,)), ((), ()))
TN = (((0,), (0,)), ((), ()))
NN = (((1,), (0,)), ((), ()))


def exact(left, right, dims=NN):
    return lax.dot_general(
        left, right, dims, precision=lax.Precision.HIGHEST, preferred_element_type=F32
    )


def narrow(left, right, dims):
    return lax.dot_general(left, right, dims, preferred_element_type=F32)


def split(x):
    high = x.astype(BF16)
    low = (x - high.astype(F32)).astype(BF16)
    return high, low


def split3(x):
    high = x.astype(BF16)
    rest = x - high.astype(F32)
    mid = rest.astype(BF16)
    low = (rest - mid.astype(F32)).astype(BF16)
    return high, mid, low


def gram_of(block):
    nb = block.shape[0]
    one, two, three = split3(block)
    first = narrow(jnp.concatenate([one, two, three], 0), one, NT)
    second = narrow(jnp.concatenate([one, two], 0), two, NT)
    third = narrow(one, three, NT)
    return (
        first[:nb]
        + (first[nb : 2 * nb] + second[:nb])
        + (first[2 * nb :] + second[nb:] + third)
    )


def cross(left, right):
    nb = left.shape[0]
    lh, ll = split(left)
    rh, rl = split(right)
    both = narrow(jnp.concatenate([lh, ll], 0), rh, NT)
    return both[:nb] + both[nb:] + narrow(lh, rl, NT)


def eliminate(tables, nb):
    rows = lax.broadcasted_iota(jnp.int32, (nb, 128), 0)
    for j in range(nb):
        done = []
        for table in tables:
            column = jnp.broadcast_to(table[:, j : j + 1], (nb, 128))
            pivot_row = table[j : j + 1, :] / column[j : j + 1, :]
            done.append(table - jnp.where(rows > j, column, 0.0) * pivot_row)
        tables = done
    return tables


def pack(square):
    total = square[0:8]
    for k in range(1, 4):
        total = total + pltpu.roll(square[8 * k : 8 * k + 8], 32 * k, 1)
    return total


def unpack(packed, lanes):
    parts = [packed] + [pltpu.roll(packed, 128 - 32 * k, 1) for k in range(1, 4)]
    return jnp.where(lanes < 32, jnp.concatenate(parts, 0), 0.0)


def wide(square):
    return jnp.concatenate([square, jnp.zeros((square.shape[0], 128 - square.shape[1]), F32)], 1)


def exchange_kernel(
    nrow, ncol,
    slab, panel, far,
    images, coefs,
    pv, sv, fv, gsend, gbuf, headbuf, pt, zout, pbuf, zsum,
    leaf3, leaf4, near, relay, twos, zown, osend, obuf, h1send, h1buf, h2send, h2buf,
    load_sem, g_ssem, g_rsem, t_ssem, t_rsem, p_ssem, p_rsem, r_ssem, r_rsem,
    a_ssem, a_rsem, f_ssem, f_rsem, o_ssem, o_rsem, h1_ssem, h1_rsem, h2_ssem, h2_rsem,
    image_sem,
):
    nb = 32
    nz = ncol // 2
    chunk = pv.shape[1] // ncol
    half = chunk // 2
    row = lax.axis_index("row")
    col = lax.axis_index("col")
    z = lax.div(col, 2)
    core = lax.rem(col, 2)
    partner = {"col": col + 1 - 2 * core}
    rows = lax.broadcasted_iota(jnp.int32, (nb, 128), 0)
    lanes = lax.broadcasted_iota(jnp.int32, (nb, 128), 1)

    def remote(src, dst, ssem, rsem, device):
        return pltpu.make_async_remote_copy(
            src_ref=src, dst_ref=dst, send_sem=ssem, recv_sem=rsem,
            device_id=device, device_id_type=MESH,
        )

    def row_peer(k):
        return lax.rem(row + k, nrow)

    def col_peer(k):
        return lax.rem(col + k, ncol)

    def z_peer(k):
        return lax.rem(z + k + nz, nz)

    def chip(k):
        return {"col": 2 * z_peer(k) + core}

    load_p = pltpu.make_async_copy(panel, pv, load_sem.at[0])
    load_s = pltpu.make_async_copy(slab, sv, load_sem.at[1])
    own = core * nz + z
    own_columns = pl.ds(pl.multiple_of(own * chunk, chunk), chunk)
    load_f = pltpu.make_async_copy(far.at[:, own_columns], fv, load_sem.at[2])
    load_p.start()
    load_s.start()
    load_f.start()

    barrier = pltpu.get_barrier_semaphore()

    @pl.loop(1, nrow)
    def _(k):
        pl.semaphore_signal(barrier, inc=1, device_id={"row": row_peer(k)}, device_id_type=MESH)

    for device in (partner, chip(1), chip(-1), chip(2), chip(-2)):
        pl.semaphore_signal(barrier, inc=1, device_id=device, device_id_type=MESH)

    load_p.wait()
    gram = jnp.zeros((nb, nb), F32)
    for g in range(ncol):
        gram = gram + gram_of(pv[:, g * chunk : (g + 1) * chunk])
    gsend[0:8, :] = pack(wide(gram))
    gsend[8:16, :] = pack(jnp.where(lanes < nb, pv[:, 0:128], 0.0))
    gbuf[row] = gsend[...]
    pt[...] = pv[...]
    pl.semaphore_wait(barrier, nrow + 4)

    head_columns = pl.ds(pl.multiple_of(col * 128, 128), 128)

    @pl.when(row == 0)
    def _():
        @pl.loop(1, nrow)
        def _(k):
            remote(pv.at[:, head_columns], headbuf, t_ssem.at[k], t_rsem, {"row": row_peer(k)}).start()

    @pl.loop(1, nrow)
    def _(k):
        remote(gsend, gbuf.at[row], g_ssem.at[k], g_rsem.at[row], {"row": row_peer(k)}).start()

    @pl.when(row == 0)
    def _():
        local_head = pltpu.make_async_copy(pv.at[:, head_columns], headbuf, load_sem.at[3])
        local_head.start()
        local_head.wait()

    load_s.wait()

    @pl.when(row != 0)
    def _():
        remote(pv.at[:, head_columns], headbuf, t_ssem.at[0], t_rsem, {"row": 0}).wait_recv()

    def produce():
        high, low = split(headbuf[...])
        weights = jnp.concatenate(
            [
                jnp.concatenate([high, high], 1),
                jnp.concatenate([low, jnp.zeros_like(low)], 1),
            ],
            0,
        )

        def product(index):
            block = sv[pl.ds(pl.multiple_of(index * chunk, chunk), chunk), :]
            sh, sl = split(block)
            both = narrow(weights, jnp.concatenate([sh, sl], 1), NT)
            return both[:nb] + both[nb:]

        def to_partner(peer):
            return remote(zout.at[peer], pbuf.at[peer], p_ssem.at[peer], p_rsem.at[peer], partner)

        def other_half(k):
            peer = z_peer(k)
            zout[peer] = product((1 - core) * nz + peer)

            @pl.when(k > 3)
            def _():
                to_partner(z_peer(k - 1)).start()

        def own_half(k):
            peer = z_peer(k)
            part = product(core * nz + peer)
            to_partner(peer).wait_recv()
            zsum[peer] = part + pbuf[peer]

        pl.loop(3, nz + 3)(other_half)
        to_partner(z_peer(nz + 2)).start()
        pl.loop(3, nz - 2)(own_half)
        pl.loop(nz - 2, nz + 3)(own_half)
        stage_one(lambda copy: copy.start())

    def stage_one(act):
        act(remote(zsum.at[z_peer(-3)], leaf3.at[0], r_ssem.at[0], r_rsem.at[0], chip(-1)))
        act(remote(zsum.at[z_peer(3)], leaf3.at[1], r_ssem.at[1], r_rsem.at[1], chip(1)))
        first = zsum.at[z_peer(4), :, pl.ds(0, half)]
        second = zsum.at[z_peer(4), :, pl.ds(half, half)]
        act(remote(first, leaf4.at[0], r_ssem.at[2], r_rsem.at[2], chip(-2)))
        act(remote(second, leaf4.at[1], r_ssem.at[3], r_rsem.at[3], chip(2)))
        act(remote(zsum.at[z_peer(-1)], near.at[0], r_ssem.at[4], r_rsem.at[4], chip(-1)))
        act(remote(zsum.at[z_peer(1)], near.at[1], r_ssem.at[5], r_rsem.at[5], chip(1)))

    def stage_two(act):
        act(remote(relay.at[0], twos.at[0], r_ssem.at[6], r_rsem.at[6], chip(-2)))
        act(remote(relay.at[1], twos.at[1], r_ssem.at[7], r_rsem.at[7], chip(2)))

    def arrived(index, slot):
        remote(slot, slot, r_ssem.at[index], r_rsem.at[index], partner).wait_recv()

    pl.when(z != 0)(produce)

    @pl.loop(1, nrow)
    def _(k):
        peer = row_peer(k)
        remote(gsend, gbuf.at[peer], g_ssem.at[k], g_rsem.at[peer], {"row": peer}).wait_recv()

    total = gbuf[0, 0:8]
    for r in range(1, nrow):
        total = total + gbuf[r, 0:8]
    table = (
        unpack(total, lanes)
        + jnp.where(lanes == rows + nb, 1.0, 0.0)
        + pltpu.roll(unpack(gbuf[0, 8:16], lanes), 2 * nb, 1)
    )
    (table,) = eliminate([table], nb)
    pivots = jnp.sum(jnp.where(lanes == rows, table, 0.0), axis=1, keepdims=True)
    table = table / jnp.sqrt(pivots)
    signs = jnp.sum(jnp.where(lanes == rows + 2 * nb, table, 0.0), axis=1, keepdims=True)
    flip = jnp.where(signs >= 0.0, -1.0, 1.0).astype(F32)
    upper = jnp.where((lanes >= rows) & (lanes < nb), table * flip, 0.0)
    correction = wide(upper[:, :nb].T)

    @pl.when(col == 0)
    def _():
        headbuf[...] = headbuf[...] - correction

    pl.when(z == 0)(produce)

    @pl.when(row == 0)
    def _():
        pt[:, 0:128] = pt[:, 0:128] - correction

    arrived(0, leaf3.at[0])
    arrived(2, leaf4.at[0])
    low_side = zsum[z_peer(-2)] + leaf3[0]
    relay[0, :, 0:half] = low_side[:, 0:half] + leaf4[0]
    relay[0, :, half:] = low_side[:, half:]
    arrived(1, leaf3.at[1])
    arrived(3, leaf4.at[1])
    high_side = zsum[z_peer(2)] + leaf3[1]
    relay[1, :, 0:half] = high_side[:, 0:half]
    relay[1, :, half:] = high_side[:, half:] + leaf4[1]
    stage_two(lambda copy: copy.start())

    load_f.wait()
    inner = cross(fv[...], pt[:, own_columns])
    for g in range(nz):
        columns = pl.ds(pl.multiple_of((core * nz + g) * chunk, chunk), chunk)
        inner = inner + cross(zsum[g], pt[:, columns])
    h1send[...] = pack(wide(inner))
    h1buf[row] = h1send[...]

    @pl.loop(1, nrow)
    def _(k):
        remote(h1send, h1buf.at[row], h1_ssem.at[k], h1_rsem.at[row], {"row": row_peer(k)}).start()

    @pl.when(row == 0)
    def _():
        extra = pltpu.make_async_copy(far.at[:, head_columns], obuf, load_sem.at[4])
        extra.start()
        head = sv.shape[1] * ncol
        ph, plow = split(pt[:, 0:head])
        sh, sl = split(sv[0:head, :])
        both = narrow(jnp.concatenate([ph, plow], 0), sh, NN)
        product = both[:nb] + both[nb:] + narrow(ph, sl, NN)
        extra.wait()
        osend[...] = product + obuf[...]
        obuf[...] = osend[...]

        @pl.loop(1, nrow)
        def _(k):
            remote(osend, obuf, o_ssem.at[k], o_rsem, {"row": row_peer(k)}).start()

    flipped_inverse = (pltpu.roll(table, 128 - nb, 1) * flip)[:, :nb]
    shifted_t = jnp.where(lanes == rows, 1.0, 0.0) - jnp.where(
        lanes < nb, pltpu.roll(table, 128 - 2 * nb, 1) * flip, 0.0
    )
    shifted = wide(shifted_t[:, :nb].T)
    augment = jnp.where(lanes == rows + nb, 1.0, 0.0)
    lower_table, upper_table = eliminate([shifted + augment, shifted_t + augment], nb)
    diagonal = jnp.sum(jnp.where(lanes == rows, upper_table, 0.0), axis=1, keepdims=True)
    lower_inverse = pltpu.roll(lower_table, 128 - nb, 1)[:, :nb]
    upper_inverse_t = (pltpu.roll(upper_table, 128 - nb, 1) / diagonal)[:, :nb]
    mixing_t = -exact(upper_inverse_t, flipped_inverse)
    second_t = -exact(lower_inverse, flipped_inverse)

    @pl.loop(1, nrow)
    def _(k):
        peer = row_peer(k)
        remote(h1send, h1buf.at[peer], h1_ssem.at[k], h1_rsem.at[peer], {"row": peer}).wait_recv()

    share = h1buf[0]
    for r in range(1, nrow):
        share = share + h1buf[r]
    h2send[...] = share
    h2buf[col] = share

    arrived(4, near.at[0])
    arrived(5, near.at[1])
    arrived(6, twos.at[0])
    arrived(7, twos.at[1])
    zown[...] = (fv[...] + zsum[z]) + (near[0] + near[1]) + (twos[0] + twos[1])

    @pl.loop(1, ncol)
    def _(k):
        remote(h2send, h2buf.at[col], h2_ssem.at[k], h2_rsem.at[col], {"col": col_peer(k)}).start()

    def slot(k):
        return images.at[core * nz + z_peer(k)]

    def half_slot(k, part):
        return images.at[core * nz + z_peer(k), :, pl.ds(part * half, half)]

    def gather(k):
        return remote(zown, slot(0), a_ssem.at[k % 8], a_rsem.at[-k % 8], chip(k))

    def got(k):
        remote(slot(k), slot(k), a_ssem.at[0], a_rsem.at[k % 8], partner).wait_recv()

    def got_half(part):
        remote(half_slot(4, part), half_slot(4, part), a_ssem.at[0], a_rsem.at[4 * part], partner).wait_recv()

    def pass_on():
        return (
            remote(slot(-2), slot(-2), a_ssem.at[3], a_rsem.at[5], chip(1)),
            remote(half_slot(-2, 0), half_slot(-2, 0), a_ssem.at[4], a_rsem.at[0], chip(2)),
            remote(slot(2), slot(2), a_ssem.at[5], a_rsem.at[3], chip(-1)),
            remote(half_slot(2, 1), half_slot(2, 1), a_ssem.at[0], a_rsem.at[4], chip(-2)),
        )

    def share_chunk(src, k):
        return remote(src, slot(k), f_ssem.at[z_peer(k)], f_rsem.at[z_peer(k)], partner)

    for k in (2, -2, 1, -1):
        gather(k).start()
    keep = pltpu.make_async_copy(zown, slot(0), image_sem)
    keep.start()
    share_chunk(zown, 0).start()
    copies = pass_on()
    got(-2)
    copies[0].start()
    copies[1].start()
    share_chunk(slot(-2), -2).start()
    got(2)
    copies[2].start()
    copies[3].start()
    share_chunk(slot(2), 2).start()
    for k in (1, -1):
        got(k)
        share_chunk(slot(k), k).start()

    own_reflectors = exact(mixing_t, headbuf[...])
    bottom = exact(second_t, own_reflectors, TN)
    kernel_t = exact(second_t, mixing_t, TN)

    @pl.when(row != 0)
    def _():
        remote(osend, obuf, o_ssem.at[0], o_rsem, {"row": 0}).wait_recv()

    own_base = exact(second_t, obuf[...])

    @pl.loop(1, ncol)
    def _(k):
        peer = col_peer(k)
        remote(h2send, h2buf.at[peer], h2_ssem.at[k], h2_rsem.at[peer], {"col": peer}).wait_recv()

    inner_total = h2buf[0]
    for c in range(1, ncol):
        inner_total = inner_total + h2buf[c]
    inner_t = unpack(inner_total, lanes)[:, :nb]
    weight_t = -0.5 * exact(exact(second_t, inner_t), kernel_t)
    own_weights = own_base + exact(weight_t, headbuf[...])
    top_part = exact(mixing_t, own_weights, TN) + exact(weight_t, own_reflectors, TN)
    coefs[0:nb, :] = top_part
    coefs[nb : 2 * nb, :] = bottom
    coefs[2 * nb : 3 * nb, :] = wide(jnp.concatenate([weight_t, second_t], 1))
    coefs[3 * nb :, :] = jnp.where(row == 0, correction, 0.0)

    for k in (3, -3):
        got(k)
        share_chunk(slot(k), k).start()
    got_half(0)
    got_half(1)
    share_chunk(slot(4), 4).start()

    @pl.loop(0, nz)
    def _(k):
        there = images.at[(1 - core) * nz + k]
        remote(there, there, f_ssem.at[k], f_rsem.at[k], partner).wait_recv()

    keep.wait()

    @pl.loop(0, nz)
    def _(k):
        remote(zout.at[k], pbuf.at[k], p_ssem.at[k], p_rsem.at[k], partner).wait_send()
        there = images.at[core * nz + k]
        remote(there, there, f_ssem.at[k], f_rsem.at[k], partner).wait_send()

    stage_one(lambda copy: copy.wait_send())
    stage_two(lambda copy: copy.wait_send())
    for k in (2, -2, 1, -1):
        gather(k).wait_send()
    for copy in copies:
        copy.wait_send()

    @pl.loop(1, nrow)
    def _(k):
        device = {"row": row_peer(k)}
        remote(gsend, gbuf.at[row], g_ssem.at[k], g_rsem.at[row], device).wait_send()
        remote(h1send, h1buf.at[row], h1_ssem.at[k], h1_rsem.at[row], device).wait_send()

    @pl.loop(1, ncol)
    def _(k):
        remote(h2send, h2buf.at[col], h2_ssem.at[k], h2_rsem.at[col], {"col": col_peer(k)}).wait_send()

    @pl.when(row == 0)
    def _():
        @pl.loop(1, nrow)
        def _(k):
            device = {"row": row_peer(k)}
            remote(pv.at[:, head_columns], headbuf, t_ssem.at[k], t_rsem, device).wait_send()
            remote(osend, obuf, o_ssem.at[k], o_rsem, device).wait_send()


def update_kernel(groups, slab, panel, images, coefs, updated, factor,
                  sv, pv, zv, cv, uv, wv, in_sem, coef_sem, out_sem):
    nb = 32
    parts = images.shape[0] // groups
    chunk = images.shape[2]
    length = parts * chunk

    def reads(g):
        span = pl.ds(pl.multiple_of(g * length, length), length)
        zs = pl.ds(g * parts, parts)
        return (
            pltpu.make_async_copy(panel.at[:, span], pv.at[:, span], in_sem.at[0, g]),
            pltpu.make_async_copy(images.at[zs], zv.at[zs], in_sem.at[1, g]),
            pltpu.make_async_copy(slab.at[span, :], sv.at[span, :], in_sem.at[2, g]),
        )

    def writes(g):
        span = pl.ds(pl.multiple_of(g * length, length), length)
        return (
            pltpu.make_async_copy(wv.at[:, span], factor.at[:, span], out_sem.at[0, g]),
            pltpu.make_async_copy(uv.at[span, :], updated.at[span, :], out_sem.at[1, g]),
        )

    load_c = pltpu.make_async_copy(coefs, cv, coef_sem)
    load_c.start()
    for g in range(groups):
        for copy in reads(g):
            copy.start()
    load_c.wait()
    bh, bl = split(cv[0 : 2 * nb, :])
    right = jnp.concatenate([bh, bl, bh], 0)
    ch, cl = split(cv[2 * nb : 3 * nb, 0 : 2 * nb])
    left = jnp.concatenate([ch, ch, cl], 1)
    for g in range(groups):
        for copy in reads(g):
            copy.wait()
        if g == 0:
            pv[:, 0:128] = pv[:, 0:128] - cv[3 * nb :, :]
        for i in range(g * parts, (g + 1) * parts):
            piece = slice(i * chunk, (i + 1) * chunk)
            xh, xl = split(jnp.concatenate([pv[:, piece], zv[i]], 0))
            wv[:, piece] = narrow(left, jnp.concatenate([xh, xl, xh], 0), NN)
            uv[piece, :] = sv[piece, :] - narrow(jnp.concatenate([xh, xh, xl], 0), right, TN)
        for copy in writes(g):
            copy.start()
    for g in range(groups):
        for copy in writes(g):
            copy.wait()


def local(nrow, ncol, slab, panel, far):
    nb, length = panel.shape
    chunk = length // ncol
    nz = ncol // 2
    anywhere = pl.BlockSpec(memory_space=pl.ANY)
    vmem = pl.BlockSpec(memory_space=pltpu.VMEM)
    dma = pltpu.SemaphoreType.DMA
    strip = pltpu.VMEM((nb, 128), F32)
    tile = pltpu.VMEM((8, 128), F32)

    def chunks(n, width=chunk):
        return pltpu.VMEM((n, nb, width), F32)

    images, coefs = pl.pallas_call(
        functools.partial(exchange_kernel, nrow, ncol),
        name="exchange",
        out_shape=(
            jax.ShapeDtypeStruct((ncol, nb, chunk), F32),
            jax.ShapeDtypeStruct((4 * nb, 128), F32),
        ),
        in_specs=[anywhere] * 3,
        out_specs=(anywhere, vmem),
        scratch_shapes=[
            pltpu.VMEM((nb, length), F32),
            pltpu.VMEM(slab.shape, F32),
            pltpu.VMEM((nb, chunk), F32),
            pltpu.VMEM((16, 128), F32),
            pltpu.VMEM((nrow, 16, 128), F32),
            strip,
            pltpu.VMEM((nb, length), F32),
            chunks(nz), chunks(nz), chunks(nz),
            chunks(2), chunks(2, chunk // 2), chunks(2), chunks(2), chunks(2),
            pltpu.VMEM((nb, chunk), F32),
            strip, strip,
            tile, pltpu.VMEM((nrow, 8, 128), F32),
            tile, pltpu.VMEM((ncol, 8, 128), F32),
            dma((5,)),
            dma((nrow,)), dma((nrow,)),
            dma((nrow,)), dma(()),
            dma((nz,)), dma((nz,)),
            dma((8,)), dma((8,)),
            dma((8,)), dma((8,)),
            dma((nz,)), dma((nz,)),
            dma((nrow,)), dma(()),
            dma((nrow,)), dma((nrow,)),
            dma((ncol,)), dma((ncol,)),
            dma(()),
        ],
        compiler_params=pltpu.CompilerParams(
            collective_id=0, has_side_effects=True, vmem_limit_bytes=60 * 2**20
        ),
    )(slab, panel, far)
    groups = 8
    return pl.pallas_call(
        functools.partial(update_kernel, groups),
        name="update",
        out_shape=(
            jax.ShapeDtypeStruct(slab.shape, F32),
            jax.ShapeDtypeStruct(panel.shape, F32),
        ),
        in_specs=[anywhere] * 4,
        out_specs=(anywhere, anywhere),
        scratch_shapes=[
            pltpu.VMEM(slab.shape, F32),
            pltpu.VMEM(panel.shape, F32),
            pltpu.VMEM((ncol, nb, chunk), F32),
            pltpu.VMEM((4 * nb, 128), F32),
            pltpu.VMEM(slab.shape, F32),
            pltpu.VMEM(panel.shape, F32),
            dma((3, groups)), dma(()), dma((2, groups)),
        ],
        compiler_params=pltpu.CompilerParams(vmem_limit_bytes=60 * 2**20),
    )(slab, panel, images, coefs)


def solution(mesh):
    sizes = dict(mesh.shape)
    body = functools.partial(local, sizes["row"], sizes["col"])
    in_specs = (P("row", "col"), P(None, "row"), P(None, "row"))
    out_specs = (P("row", "col"), P(None, "row"))
    return jax.shard_map(body, mesh=mesh, in_specs=in_specs, out_specs=out_specs, check_vma=False)
```

time: 66.5 us -> 54.6 us (0.82)
  the two profiles are of different devices: /device:TPU:37 before, /device:TPU:1 now
where the time goes in v2:
time: 54.6 us; the launch traced here: 54.4 us
  Pallas kernels  53.8 us (99%)
  between operations  0.64 us (1%)
    pallas_call x1, Pallas kernels, local(): pl.pallas_call(functools.partial(exchange_kernel, nrow, ncol), name='exch...  46.9 us
    pallas_call x1, Pallas kernels, local(): pl.pallas_call(functools.partial(update_kernel, groups), name='update', o...  6.91 us

profile of v2, /device:TPU:1, one launch (start us, length us, event | category | flops | bytes accessed | tf_op | source)
XLA Modules:
  0.0 54.4 jit_solution(10572444029060227036)
XLA Ops:
  0.6 46.9 %exchange.1 = (f32[16,32,512]{2,1,0:T(8,128)}, f32[128,128]{1,0:T(8,128)}) custom-call(f32[8192,128]{1,0:T(8,128)} %slab.3, f32[32,8192]{1,0:T(8,128)} %panel.3, f32[32,8192]{1,0:T(8,128)} %far.1), custom_call_target="tpu_custom_call" | custom-call | tf_op jit(solution)/shard_map/exchange/pallas_call | solution.py:527
  47.5 6.9 %update.1 = (f32[8192,128]{1,0:T(8,128)}, f32[32,8192]{1,0:T(8,128)}) custom-call(f32[8192,128]{1,0:T(8,128)} %slab.3, f32[32,8192]{1,0:T(8,128)} %panel.3, f32[16,32,512]{2,1,0:T(8,128)} %get-tuple-element.4.images, f32[128,128]{1,0:T(8,128)} %get-tuple-element.5.coefs), custom_call_target="tpu_custom_call" | custom-call | tf_op jit(solution)/shard_map/update/pallas_call | solution.py:567

commit v3 on v2

--- a/solution.py
+++ b/solution.py
@@ -116,6 +116,10 @@
             device_id=device, device_id_type=MESH,
         )
 
+    def others(buffer, n, ssem, rsem):
+        slots = buffer.at[pl.ds(0, n - 1)]
+        return remote(slots, slots, ssem, rsem, partner)
+
     def row_peer(k):
         return lax.rem(row + k, nrow)
 
@@ -160,13 +164,11 @@
 
     @pl.when(row == 0)
     def _():
-        @pl.loop(1, nrow)
-        def _(k):
-            remote(pv.at[:, head_columns], headbuf, t_ssem.at[k], t_rsem, {"row": row_peer(k)}).start()
-
-    @pl.loop(1, nrow)
-    def _(k):
-        remote(gsend, gbuf.at[row], g_ssem.at[k], g_rsem.at[row], {"row": row_peer(k)}).start()
+        for k in range(1, nrow):
+            remote(pv.at[:, head_columns], headbuf, t_ssem, t_rsem, {"row": row_peer(k)}).start()
+
+    for k in range(1, nrow):
+        remote(gsend, gbuf.at[row], g_ssem, g_rsem, {"row": row_peer(k)}).start()
 
     @pl.when(row == 0)
     def _():
@@ -178,7 +180,7 @@
 
     @pl.when(row != 0)
     def _():
-        remote(pv.at[:, head_columns], headbuf, t_ssem.at[0], t_rsem, {"row": 0}).wait_recv()
+        remote(headbuf, headbuf, t_ssem, t_rsem, {"row": 0}).wait_recv()
 
     def produce():
         high, low = split(headbuf[...])
@@ -197,7 +199,7 @@
             return both[:nb] + both[nb:]
 
         def to_partner(peer):
-            return remote(zout.at[peer], pbuf.at[peer], p_ssem.at[peer], p_rsem.at[peer], partner)
+            return remote(zout.at[peer], pbuf.at[peer], p_ssem, p_rsem.at[peer], partner)
 
         def other_half(k):
             peer = z_peer(k)
@@ -238,10 +240,7 @@
 
     pl.when(z != 0)(produce)
 
-    @pl.loop(1, nrow)
-    def _(k):
-        peer = row_peer(k)
-        remote(gsend, gbuf.at[peer], g_ssem.at[k], g_rsem.at[peer], {"row": peer}).wait_recv()
+    others(gbuf, nrow, g_ssem, g_rsem).wait_recv()
 
     total = gbuf[0, 0:8]
     for r in range(1, nrow):
@@ -289,9 +288,8 @@
     h1send[...] = pack(wide(inner))
     h1buf[row] = h1send[...]
 
-    @pl.loop(1, nrow)
-    def _(k):
-        remote(h1send, h1buf.at[row], h1_ssem.at[k], h1_rsem.at[row], {"row": row_peer(k)}).start()
+    for k in range(1, nrow):
+        remote(h1send, h1buf.at[row], h1_ssem, h1_rsem, {"row": row_peer(k)}).start()
 
     @pl.when(row == 0)
     def _():
@@ -306,9 +304,8 @@
         osend[...] = product + obuf[...]
         obuf[...] = osend[...]
 
-        @pl.loop(1, nrow)
-        def _(k):
-            remote(osend, obuf, o_ssem.at[k], o_rsem, {"row": row_peer(k)}).start()
+        for k in range(1, nrow):
+            remote(osend, obuf, o_ssem, o_rsem, {"row": row_peer(k)}).start()
 
     flipped_inverse = (pltpu.roll(table, 128 - nb, 1) * flip)[:, :nb]
     shifted_t = jnp.where(lanes == rows, 1.0, 0.0) - jnp.where(
@@ -323,10 +320,7 @@
     mixing_t = -exact(upper_inverse_t, flipped_inverse)
     second_t = -exact(lower_inverse, flipped_inverse)
 
-    @pl.loop(1, nrow)
-    def _(k):
-        peer = row_peer(k)
-        remote(h1send, h1buf.at[peer], h1_ssem.at[k], h1_rsem.at[peer], {"row": peer}).wait_recv()
+    others(h1buf, nrow, h1_ssem, h1_rsem).wait_recv()
 
     share = h1buf[0]
     for r in range(1, nrow):
@@ -340,9 +334,8 @@
     arrived(7, twos.at[1])
     zown[...] = (fv[...] + zsum[z]) + (near[0] + near[1]) + (twos[0] + twos[1])
 
-    @pl.loop(1, ncol)
-    def _(k):
-        remote(h2send, h2buf.at[col], h2_ssem.at[k], h2_rsem.at[col], {"col": col_peer(k)}).start()
+    for k in range(1, ncol):
+        remote(h2send, h2buf.at[col], h2_ssem, h2_rsem, {"col": col_peer(k)}).start()
 
     def slot(k):
         return images.at[core * nz + z_peer(k)]
@@ -368,7 +361,7 @@
         )
 
     def share_chunk(src, k):
-        return remote(src, slot(k), f_ssem.at[z_peer(k)], f_rsem.at[z_peer(k)], partner)
+        return remote(src, slot(k), f_ssem, f_rsem, partner)
 
     for k in (2, -2, 1, -1):
         gather(k).start()
@@ -394,14 +387,11 @@
 
     @pl.when(row != 0)
     def _():
-        remote(osend, obuf, o_ssem.at[0], o_rsem, {"row": 0}).wait_recv()
+        remote(obuf, obuf, o_ssem, o_rsem, {"row": 0}).wait_recv()
 
     own_base = exact(second_t, obuf[...])
 
-    @pl.loop(1, ncol)
-    def _(k):
-        peer = col_peer(k)
-        remote(h2send, h2buf.at[peer], h2_ssem.at[k], h2_rsem.at[peer], {"col": peer}).wait_recv()
+    others(h2buf, ncol, h2_ssem, h2_rsem).wait_recv()
 
     inner_total = h2buf[0]
     for c in range(1, ncol):
@@ -422,88 +412,59 @@
     got_half(1)
     share_chunk(slot(4), 4).start()
 
-    @pl.loop(0, nz)
-    def _(k):
-        there = images.at[(1 - core) * nz + k]
-        remote(there, there, f_ssem.at[k], f_rsem.at[k], partner).wait_recv()
+    theirs = images.at[pl.ds((1 - core) * nz, nz)]
+    remote(theirs, theirs, f_ssem, f_rsem, partner).wait_recv()
 
     keep.wait()
 
-    @pl.loop(0, nz)
-    def _(k):
-        remote(zout.at[k], pbuf.at[k], p_ssem.at[k], p_rsem.at[k], partner).wait_send()
-        there = images.at[core * nz + k]
-        remote(there, there, f_ssem.at[k], f_rsem.at[k], partner).wait_send()
-
+    remote(zout, pbuf, p_ssem, p_rsem.at[0], partner).wait_send()
+    mine = images.at[pl.ds(0, nz)]
+    remote(mine, mine, f_ssem, f_rsem, partner).wait_send()
     stage_one(lambda copy: copy.wait_send())
     stage_two(lambda copy: copy.wait_send())
     for k in (2, -2, 1, -1):
         gather(k).wait_send()
     for copy in copies:
         copy.wait_send()
-
-    @pl.loop(1, nrow)
-    def _(k):
-        device = {"row": row_peer(k)}
-        remote(gsend, gbuf.at[row], g_ssem.at[k], g_rsem.at[row], device).wait_send()
-        remote(h1send, h1buf.at[row], h1_ssem.at[k], h1_rsem.at[row], device).wait_send()
-
-    @pl.loop(1, ncol)
-    def _(k):
-        remote(h2send, h2buf.at[col], h2_ssem.at[k], h2_rsem.at[col], {"col": col_peer(k)}).wait_send()
+    others(gbuf, nrow, g_ssem, g_rsem).wait_send()
+    others(h1buf, nrow, h1_ssem, h1_rsem).wait_send()
+    others(h2buf, ncol, h2_ssem, h2_rsem).wait_send()
 
     @pl.when(row == 0)
     def _():
-        @pl.loop(1, nrow)
-        def _(k):
-            device = {"row": row_peer(k)}
-            remote(pv.at[:, head_columns], headbuf, t_ssem.at[k], t_rsem, device).wait_send()
-            remote(osend, obuf, o_ssem.at[k], o_rsem, device).wait_send()
-
-
-def update_kernel(groups, slab, panel, images, coefs, updated, factor,
-                  sv, pv, zv, cv, uv, wv, in_sem, coef_sem, out_sem):
+        heads = pv.at[:, pl.ds(0, 128 * (nrow - 1))]
+        remote(heads, heads, t_ssem, t_rsem, partner).wait_send()
+        remote(heads, heads, o_ssem, o_rsem, partner).wait_send()
+
+
+def update_kernel(groups, slab, panel, images, coefs, updated, factor, uv, wv, out_sem):
     nb = 32
     parts = images.shape[0] // groups
     chunk = images.shape[2]
     length = parts * chunk
 
-    def reads(g):
-        span = pl.ds(pl.multiple_of(g * length, length), length)
-        zs = pl.ds(g * parts, parts)
-        return (
-            pltpu.make_async_copy(panel.at[:, span], pv.at[:, span], in_sem.at[0, g]),
-            pltpu.make_async_copy(images.at[zs], zv.at[zs], in_sem.at[1, g]),
-            pltpu.make_async_copy(slab.at[span, :], sv.at[span, :], in_sem.at[2, g]),
-        )
-
     def writes(g):
-        span = pl.ds(pl.multiple_of(g * length, length), length)
+        span = pl.ds(g * length, length)
         return (
             pltpu.make_async_copy(wv.at[:, span], factor.at[:, span], out_sem.at[0, g]),
             pltpu.make_async_copy(uv.at[span, :], updated.at[span, :], out_sem.at[1, g]),
         )
 
-    load_c = pltpu.make_async_copy(coefs, cv, coef_sem)
-    load_c.start()
-    for g in range(groups):
-        for copy in reads(g):
-            copy.start()
-    load_c.wait()
-    bh, bl = split(cv[0 : 2 * nb, :])
+    bh, bl = split(coefs[0 : 2 * nb, :])
     right = jnp.concatenate([bh, bl, bh], 0)
-    ch, cl = split(cv[2 * nb : 3 * nb, 0 : 2 * nb])
+    ch, cl = split(coefs[2 * nb : 3 * nb, 0 : 2 * nb])
     left = jnp.concatenate([ch, ch, cl], 1)
     for g in range(groups):
-        for copy in reads(g):
-            copy.wait()
-        if g == 0:
-            pv[:, 0:128] = pv[:, 0:128] - cv[3 * nb :, :]
         for i in range(g * parts, (g + 1) * parts):
             piece = slice(i * chunk, (i + 1) * chunk)
-            xh, xl = split(jnp.concatenate([pv[:, piece], zv[i]], 0))
+            columns = panel[:, piece]
+            if i == 0:
+                columns = jnp.concatenate(
+                    [columns[:, 0:128] - coefs[3 * nb :, :], columns[:, 128:]], 1
+                )
+            xh, xl = split(jnp.concatenate([columns, images[i]], 0))
             wv[:, piece] = narrow(left, jnp.concatenate([xh, xl, xh], 0), NN)
-            uv[piece, :] = sv[piece, :] - narrow(jnp.concatenate([xh, xh, xl], 0), right, TN)
+            uv[piece, :] = slab[piece, :] - narrow(jnp.concatenate([xh, xh, xl], 0), right, TN)
         for copy in writes(g):
             copy.start()
     for g in range(groups):
@@ -548,22 +509,22 @@
             tile, pltpu.VMEM((nrow, 8, 128), F32),
             tile, pltpu.VMEM((ncol, 8, 128), F32),
             dma((5,)),
-            dma((nrow,)), dma((nrow,)),
-            dma((nrow,)), dma(()),
-            dma((nz,)), dma((nz,)),
+            dma(()), dma(()),
+            dma(()), dma(()),
+            dma(()), dma((nz,)),
             dma((8,)), dma((8,)),
             dma((8,)), dma((8,)),
-            dma((nz,)), dma((nz,)),
-            dma((nrow,)), dma(()),
-            dma((nrow,)), dma((nrow,)),
-            dma((ncol,)), dma((ncol,)),
+            dma(()), dma(()),
+            dma(()), dma(()),
+            dma(()), dma(()),
+            dma(()), dma(()),
             dma(()),
         ],
         compiler_params=pltpu.CompilerParams(
-            collective_id=0, has_side_effects=True, vmem_limit_bytes=60 * 2**20
+            collective_id=0, has_side_effects=True, vmem_limit_bytes=24 * 2**20
         ),
-    )(slab, panel, far)
-    groups = 8
+    )(*(pltpu.with_memory_space_constraint(array, pltpu.HBM) for array in (slab, panel, far)))
+    groups = 4
     return pl.pallas_call(
         functools.partial(update_kernel, groups),
         name="update",
@@ -571,18 +532,14 @@
             jax.ShapeDtypeStruct(slab.shape, F32),
             jax.ShapeDtypeStruct(panel.shape, F32),
         ),
-        in_specs=[anywhere] * 4,
+        in_specs=[vmem] * 4,
         out_specs=(anywhere, anywhere),
         scratch_shapes=[
             pltpu.VMEM(slab.shape, F32),
             pltpu.VMEM(panel.shape, F32),
-            pltpu.VMEM((ncol, nb, chunk), F32),
-            pltpu.VMEM((4 * nb, 128), F32),
-            pltpu.VMEM(slab.shape, F32),
-            pltpu.VMEM(panel.shape, F32),
-            dma((3, groups)), dma(()), dma((2, groups)),
+            dma((2, groups)),
         ],
-        compiler_params=pltpu.CompilerParams(vmem_limit_bytes=60 * 2**20),
+        compiler_params=pltpu.CompilerParams(vmem_limit_bytes=24 * 2**20),
     )(slab, panel, images, coefs)
 
 

time: 54.6 us -> 47.7 us (0.87)
  Pallas kernels: 53.8 us -> 46.9 us
    pallas_call x1, Pallas kernels: 6.91 us -> 3.03 us  [local(): pl.pallas_call(functools.partial(update_kernel, groups), name='update', o...]
    pallas_call x1, Pallas kernels: 46.9 us -> 43.9 us  [local(): pl.pallas_call(functools.partial(exchange_kernel, nrow, ncol), name='exch...]
where the time goes in v3:
time: 47.7 us; the launch traced here: 47.6 us
  Pallas kernels  46.9 us (98%)
  between operations  0.67 us (1%)
    pallas_call x1, Pallas kernels, local(): pl.pallas_call(functools.partial(exchange_kernel, nrow, ncol), name='exch...  43.9 us
    pallas_call x1, Pallas kernels, local(): pl.pallas_call(functools.partial(update_kernel, groups), name='update', o...  3.03 us

profile of v3, /device:TPU:1, one launch (start us, length us, event | category | flops | bytes accessed | tf_op | source)
XLA Modules:
  0.0 47.6 jit_solution(13798340279975530377)
XLA Ops:
  0.6 0.0 copy-start.1
  0.6 0.0 copy-start
  0.6 43.9 %exchange.1 = (f32[16,32,512]{2,1,0:T(8,128)S(1)}, f32[128,128]{1,0:T(8,128)S(1)}) custom-call(f32[8192,128]{1,0:T(8,128)} %slab.3, f32[32,8192]{1,0:T(8,128)} %panel.3, f32[32,8192]{1,0:T(8,128)} %far.1), custom_call_target="tpu_custom_call" | custom-call | tf_op jit(solution)/shard_map/exchange/pallas_call | solution.py:488
  44.6 0.0 copy-done.1
  44.6 0.0 copy-done
  44.6 3.0 %update.1 = (f32[8192,128]{1,0:T(8,128)}, f32[32,8192]{1,0:T(8,128)}) custom-call(f32[8192,128]{1,0:T(8,128)S(1)} %copy-done, f32[32,8192]{1,0:T(8,128)S(1)} %copy-done.1, f32[16,32,512]{2,1,0:T(8,128)S(1)} %get-tuple-element.4.images, f32[128,128]{1,0:T(8,128)S(1)} %get-tuple-element.5.coefs), custom_call_target="tpu_custom_call" | custom-call | tf_op jit(solution)/shard_map/update/pallas_call | solution.py:528
Async XLA Ops:
  0.6 43.9 %copy-start.1 = (f32[32,8192]{1,0:T(8,128)S(1)}, f32[32,8192]{1,0:T(8,128)}, u32[]{:S(2)}) copy-start(f32[32,8192]{1,0:T(8,128)} %panel.3) | copy-start | bytes 3145732
  0.6 43.9 %copy-start = (f32[8192,128]{1,0:T(8,128)S(1)}, f32[8192,128]{1,0:T(8,128)}, u32[]{:S(2)}) copy-start(f32[8192,128]{1,0:T(8,128)} %slab.3) | copy-start | bytes 12582916

commit v4 on v3

--- a/solution.py
+++ b/solution.py
@@ -62,12 +62,19 @@
 
 def eliminate(tables, nb):
     rows = lax.broadcasted_iota(jnp.int32, (nb, 128), 0)
-    for j in range(nb):
+    for j in range(0, nb, 2):
         done = []
         for table in tables:
             column = jnp.broadcast_to(table[:, j : j + 1], (nb, 128))
-            pivot_row = table[j : j + 1, :] / column[j : j + 1, :]
-            done.append(table - jnp.where(rows > j, column, 0.0) * pivot_row)
+            following = jnp.broadcast_to(table[:, j + 1 : j + 2], (nb, 128))
+            pivot = column[j : j + 1, :]
+            pivot_row = table[j : j + 1, :] / pivot
+            below = jnp.where(rows > j, column, 0.0)
+            following = following - below * (following[j : j + 1, :] / pivot)
+            next_row = table[j + 1 : j + 2, :] - column[j + 1 : j + 2, :] * pivot_row
+            next_row = next_row / following[j + 1 : j + 2, :]
+            after = jnp.where(rows > j + 1, following, 0.0)
+            done.append(table - below * pivot_row - after * next_row)
         tables = done
     return tables
 
@@ -93,10 +100,10 @@
     slab, panel, far,
     images, coefs,
     pv, sv, fv, gsend, gbuf, headbuf, pt, zout, pbuf, zsum,
-    leaf3, leaf4, near, relay, twos, zown, osend, obuf, h1send, h1buf, h2send, h2buf,
+    leaf3, leaf4, near, relay, twos, zown, osend, obuf, h1send, h1buf, h2send, h2buf, pairsend, pairbuf,
     load_sem, g_ssem, g_rsem, t_ssem, t_rsem, p_ssem, p_rsem, r_ssem, r_rsem,
     a_ssem, a_rsem, f_ssem, f_rsem, o_ssem, o_rsem, h1_ssem, h1_rsem, h2_ssem, h2_rsem,
-    image_sem,
+    pair_sem, image_sem,
 ):
     nb = 32
     nz = ncol // 2
@@ -123,9 +130,6 @@
     def row_peer(k):
         return lax.rem(row + k, nrow)
 
-    def col_peer(k):
-        return lax.rem(col + k, ncol)
-
     def z_peer(k):
         return lax.rem(z + k + nz, nz)
 
@@ -215,19 +219,23 @@
             to_partner(peer).wait_recv()
             zsum[peer] = part + pbuf[peer]
 
-        pl.loop(3, nz + 3)(other_half)
+        pl.loop(3, nz)(other_half)
+        pl.loop(3, nz - 2)(own_half)
+        leaves(lambda copy: copy.start())
+        pl.loop(nz, nz + 3)(other_half)
         to_partner(z_peer(nz + 2)).start()
-        pl.loop(3, nz - 2)(own_half)
         pl.loop(nz - 2, nz + 3)(own_half)
-        stage_one(lambda copy: copy.start())
-
-    def stage_one(act):
+        nears(lambda copy: copy.start())
+
+    def leaves(act):
         act(remote(zsum.at[z_peer(-3)], leaf3.at[0], r_ssem.at[0], r_rsem.at[0], chip(-1)))
         act(remote(zsum.at[z_peer(3)], leaf3.at[1], r_ssem.at[1], r_rsem.at[1], chip(1)))
         first = zsum.at[z_peer(4), :, pl.ds(0, half)]
         second = zsum.at[z_peer(4), :, pl.ds(half, half)]
         act(remote(first, leaf4.at[0], r_ssem.at[2], r_rsem.at[2], chip(-2)))
         act(remote(second, leaf4.at[1], r_ssem.at[3], r_rsem.at[3], chip(2)))
+
+    def nears(act):
         act(remote(zsum.at[z_peer(-1)], near.at[0], r_ssem.at[4], r_rsem.at[4], chip(-1)))
         act(remote(zsum.at[z_peer(1)], near.at[1], r_ssem.at[5], r_rsem.at[5], chip(1)))
 
@@ -320,22 +328,11 @@
     mixing_t = -exact(upper_inverse_t, flipped_inverse)
     second_t = -exact(lower_inverse, flipped_inverse)
 
-    others(h1buf, nrow, h1_ssem, h1_rsem).wait_recv()
-
-    share = h1buf[0]
-    for r in range(1, nrow):
-        share = share + h1buf[r]
-    h2send[...] = share
-    h2buf[col] = share
-
     arrived(4, near.at[0])
     arrived(5, near.at[1])
     arrived(6, twos.at[0])
     arrived(7, twos.at[1])
     zown[...] = (fv[...] + zsum[z]) + (near[0] + near[1]) + (twos[0] + twos[1])
-
-    for k in range(1, ncol):
-        remote(h2send, h2buf.at[col], h2_ssem, h2_rsem, {"col": col_peer(k)}).start()
 
     def slot(k):
         return images.at[core * nz + z_peer(k)]
@@ -369,6 +366,15 @@
     keep.start()
     share_chunk(zown, 0).start()
     copies = pass_on()
+
+    others(h1buf, nrow, h1_ssem, h1_rsem).wait_recv()
+    share = h1buf[0]
+    for r in range(1, nrow):
+        share = share + h1buf[r]
+    pairsend[...] = share
+    pair = remote(pairsend, pairbuf, pair_sem.at[0], pair_sem.at[1], partner)
+    pair.start()
+
     got(-2)
     copies[0].start()
     copies[1].start()
@@ -377,6 +383,14 @@
     copies[2].start()
     copies[3].start()
     share_chunk(slot(2), 2).start()
+
+    pair.wait_recv()
+    share = share + pairbuf[...]
+    h2send[...] = share
+    h2buf[z] = share
+    for k in range(1, nz):
+        remote(h2send, h2buf.at[z], h2_ssem, h2_rsem, chip(k)).start()
+
     for k in (1, -1):
         got(k)
         share_chunk(slot(k), k).start()
@@ -391,10 +405,17 @@
 
     own_base = exact(second_t, obuf[...])
 
-    others(h2buf, ncol, h2_ssem, h2_rsem).wait_recv()
+    for k in (3, -3):
+        got(k)
+        share_chunk(slot(k), k).start()
+    got_half(0)
+    got_half(1)
+    share_chunk(slot(4), 4).start()
+
+    others(h2buf, nz, h2_ssem, h2_rsem).wait_recv()
 
     inner_total = h2buf[0]
-    for c in range(1, ncol):
+    for c in range(1, nz):
         inner_total = inner_total + h2buf[c]
     inner_t = unpack(inner_total, lanes)[:, :nb]
     weight_t = -0.5 * exact(exact(second_t, inner_t), kernel_t)
@@ -405,13 +426,6 @@
     coefs[2 * nb : 3 * nb, :] = wide(jnp.concatenate([weight_t, second_t], 1))
     coefs[3 * nb :, :] = jnp.where(row == 0, correction, 0.0)
 
-    for k in (3, -3):
-        got(k)
-        share_chunk(slot(k), k).start()
-    got_half(0)
-    got_half(1)
-    share_chunk(slot(4), 4).start()
-
     theirs = images.at[pl.ds((1 - core) * nz, nz)]
     remote(theirs, theirs, f_ssem, f_rsem, partner).wait_recv()
 
@@ -420,7 +434,8 @@
     remote(zout, pbuf, p_ssem, p_rsem.at[0], partner).wait_send()
     mine = images.at[pl.ds(0, nz)]
     remote(mine, mine, f_ssem, f_rsem, partner).wait_send()
-    stage_one(lambda copy: copy.wait_send())
+    leaves(lambda copy: copy.wait_send())
+    nears(lambda copy: copy.wait_send())
     stage_two(lambda copy: copy.wait_send())
     for k in (2, -2, 1, -1):
         gather(k).wait_send()
@@ -428,7 +443,8 @@
         copy.wait_send()
     others(gbuf, nrow, g_ssem, g_rsem).wait_send()
     others(h1buf, nrow, h1_ssem, h1_rsem).wait_send()
-    others(h2buf, ncol, h2_ssem, h2_rsem).wait_send()
+    others(h2buf, nz, h2_ssem, h2_rsem).wait_send()
+    pair.wait_send()
 
     @pl.when(row == 0)
     def _():
@@ -507,7 +523,8 @@
             pltpu.VMEM((nb, chunk), F32),
             strip, strip,
             tile, pltpu.VMEM((nrow, 8, 128), F32),
-            tile, pltpu.VMEM((ncol, 8, 128), F32),
+            tile, pltpu.VMEM((nz, 8, 128), F32),
+            tile, tile,
             dma((5,)),
             dma(()), dma(()),
             dma(()), dma(()),
@@ -518,7 +535,7 @@
             dma(()), dma(()),
             dma(()), dma(()),
             dma(()), dma(()),
-            dma(()),
+            dma((2,)), dma(()),
         ],
         compiler_params=pltpu.CompilerParams(
             collective_id=0, has_side_effects=True, vmem_limit_bytes=24 * 2**20

time: 47.7 us -> 44.3 us (0.929)
  Pallas kernels: 46.9 us -> 43.5 us
    pallas_call x1, Pallas kernels: 43.9 us -> 40.4 us  [local(): pl.pallas_call(functools.partial(exchange_kernel, nrow, ncol), name='exch...]
where the time goes in v4:
time: 44.3 us; the launch traced here: 44.1 us
  Pallas kernels  43.5 us (98%)
  between operations  0.67 us (2%)
    pallas_call x1, Pallas kernels, local(): pl.pallas_call(functools.partial(exchange_kernel, nrow, ncol), name='exch...  40.4 us
    pallas_call x1, Pallas kernels, local(): pl.pallas_call(functools.partial(update_kernel, groups), name='update', o...  3.03 us

profile of v4, /device:TPU:1, one launch (start us, length us, event | category | flops | bytes accessed | tf_op | source)
XLA Modules:
  0.0 44.1 jit_solution(4881277926538077986)
XLA Ops:
  0.6 0.0 copy-start.1
  0.6 0.0 copy-start
  0.6 40.4 %exchange.1 = (f32[16,32,512]{2,1,0:T(8,128)S(1)}, f32[128,128]{1,0:T(8,128)S(1)}) custom-call(f32[8192,128]{1,0:T(8,128)} %slab.3, f32[32,8192]{1,0:T(8,128)} %panel.3, f32[32,8192]{1,0:T(8,128)} %far.1), custom_call_target="tpu_custom_call" | custom-call | tf_op jit(solution)/shard_map/exchange/pallas_call | solution.py:504
  41.1 0.0 copy-done.1
  41.1 0.0 copy-done
  41.1 3.0 %update.1 = (f32[8192,128]{1,0:T(8,128)}, f32[32,8192]{1,0:T(8,128)}) custom-call(f32[8192,128]{1,0:T(8,128)S(1)} %copy-done, f32[32,8192]{1,0:T(8,128)S(1)} %copy-done.1, f32[16,32,512]{2,1,0:T(8,128)S(1)} %get-tuple-element.4.images, f32[128,128]{1,0:T(8,128)S(1)} %get-tuple-element.5.coefs), custom_call_target="tpu_custom_call" | custom-call | tf_op jit(solution)/shard_map/update/pallas_call | solution.py:545
Async XLA Ops:
  0.6 40.5 %copy-start.1 = (f32[32,8192]{1,0:T(8,128)S(1)}, f32[32,8192]{1,0:T(8,128)}, u32[]{:S(2)}) copy-start(f32[32,8192]{1,0:T(8,128)} %panel.3) | copy-start | bytes 3145732
  0.6 40.5 %copy-start = (f32[8192,128]{1,0:T(8,128)S(1)}, f32[8192,128]{1,0:T(8,128)}, u32[]{:S(2)}) copy-start(f32[8192,128]{1,0:T(8,128)} %slab.3) | copy-start | bytes 12582916

commit v5 on v4

--- a/solution.py
+++ b/solution.py
@@ -166,16 +166,13 @@
 
     head_columns = pl.ds(pl.multiple_of(col * 128, 128), 128)
 
+    for k in range(1, nrow):
+        remote(gsend, gbuf.at[row], g_ssem, g_rsem, {"row": row_peer(k)}).start()
+
     @pl.when(row == 0)
     def _():
         for k in range(1, nrow):
             remote(pv.at[:, head_columns], headbuf, t_ssem, t_rsem, {"row": row_peer(k)}).start()
-
-    for k in range(1, nrow):
-        remote(gsend, gbuf.at[row], g_ssem, g_rsem, {"row": row_peer(k)}).start()
-
-    @pl.when(row == 0)
-    def _():
         local_head = pltpu.make_async_copy(pv.at[:, head_columns], headbuf, load_sem.at[3])
         local_head.start()
         local_head.wait()
@@ -208,10 +205,7 @@
         def other_half(k):
             peer = z_peer(k)
             zout[peer] = product((1 - core) * nz + peer)
-
-            @pl.when(k > 3)
-            def _():
-                to_partner(z_peer(k - 1)).start()
+            to_partner(peer).start()
 
         def own_half(k):
             peer = z_peer(k)
@@ -223,7 +217,6 @@
         pl.loop(3, nz - 2)(own_half)
         leaves(lambda copy: copy.start())
         pl.loop(nz, nz + 3)(other_half)
-        to_partner(z_peer(nz + 2)).start()
         pl.loop(nz - 2, nz + 3)(own_half)
         nears(lambda copy: copy.start())
 
@@ -239,9 +232,10 @@
         act(remote(zsum.at[z_peer(-1)], near.at[0], r_ssem.at[4], r_rsem.at[4], chip(-1)))
         act(remote(zsum.at[z_peer(1)], near.at[1], r_ssem.at[5], r_rsem.at[5], chip(1)))
 
-    def stage_two(act):
-        act(remote(relay.at[0], twos.at[0], r_ssem.at[6], r_rsem.at[6], chip(-2)))
-        act(remote(relay.at[1], twos.at[1], r_ssem.at[7], r_rsem.at[7], chip(2)))
+    stage_two = (
+        remote(relay.at[0], twos.at[0], r_ssem.at[6], r_rsem.at[6], chip(-2)),
+        remote(relay.at[1], twos.at[1], r_ssem.at[7], r_rsem.at[7], chip(2)),
+    )
 
     def arrived(index, slot):
         remote(slot, slot, r_ssem.at[index], r_rsem.at[index], partner).wait_recv()
@@ -281,12 +275,13 @@
     low_side = zsum[z_peer(-2)] + leaf3[0]
     relay[0, :, 0:half] = low_side[:, 0:half] + leaf4[0]
     relay[0, :, half:] = low_side[:, half:]
+    stage_two[0].start()
     arrived(1, leaf3.at[1])
     arrived(3, leaf4.at[1])
     high_side = zsum[z_peer(2)] + leaf3[1]
     relay[1, :, 0:half] = high_side[:, 0:half]
     relay[1, :, half:] = high_side[:, half:] + leaf4[1]
-    stage_two(lambda copy: copy.start())
+    stage_two[1].start()
 
     load_f.wait()
     inner = cross(fv[...], pt[:, own_columns])
@@ -340,33 +335,41 @@
     def half_slot(k, part):
         return images.at[core * nz + z_peer(k), :, pl.ds(part * half, half)]
 
-    def gather(k):
-        return remote(zown, slot(0), a_ssem.at[k % 8], a_rsem.at[-k % 8], chip(k))
-
-    def got(k):
-        remote(slot(k), slot(k), a_ssem.at[0], a_rsem.at[k % 8], partner).wait_recv()
-
-    def got_half(part):
-        remote(half_slot(4, part), half_slot(4, part), a_ssem.at[0], a_rsem.at[4 * part], partner).wait_recv()
-
-    def pass_on():
-        return (
-            remote(slot(-2), slot(-2), a_ssem.at[3], a_rsem.at[5], chip(1)),
-            remote(half_slot(-2, 0), half_slot(-2, 0), a_ssem.at[4], a_rsem.at[0], chip(2)),
-            remote(slot(2), slot(2), a_ssem.at[5], a_rsem.at[3], chip(-1)),
-            remote(half_slot(2, 1), half_slot(2, 1), a_ssem.at[0], a_rsem.at[4], chip(-2)),
-        )
+    def half_own(part):
+        return zown.at[:, pl.ds(part * half, half)]
+
+    def got(ref, n):
+        remote(ref, ref, a_ssem.at[0], a_rsem.at[n], partner).wait_recv()
+
+    def onward(k, part, n, m, device):
+        piece = half_slot(k, part)
+        return remote(piece, piece, a_ssem.at[n], a_rsem.at[m], device)
+
+    gather = (
+        remote(half_own(0), half_slot(0, 0), a_ssem.at[0], a_rsem.at[0], chip(2)),
+        remote(half_own(1), half_slot(0, 1), a_ssem.at[1], a_rsem.at[3], chip(-2)),
+        remote(half_own(1), half_slot(0, 1), a_ssem.at[2], a_rsem.at[1], chip(2)),
+        remote(half_own(0), half_slot(0, 0), a_ssem.at[3], a_rsem.at[2], chip(-2)),
+        remote(zown, slot(0), a_ssem.at[4], a_rsem.at[4], chip(1)),
+        remote(zown, slot(0), a_ssem.at[5], a_rsem.at[5], chip(-1)),
+    )
+    copies = (
+        onward(-2, 0, 6, 10, chip(2)),
+        onward(-2, 0, 7, 6, chip(1)),
+        onward(2, 1, 8, 11, chip(-2)),
+        onward(2, 1, 9, 9, chip(-1)),
+        onward(-2, 1, 10, 7, chip(1)),
+        onward(2, 0, 11, 8, chip(-1)),
+    )
 
     def share_chunk(src, k):
         return remote(src, slot(k), f_ssem, f_rsem, partner)
 
-    for k in (2, -2, 1, -1):
-        gather(k).start()
+    for copy in gather:
+        copy.start()
     keep = pltpu.make_async_copy(zown, slot(0), image_sem)
     keep.start()
     share_chunk(zown, 0).start()
-    copies = pass_on()
-
     others(h1buf, nrow, h1_ssem, h1_rsem).wait_recv()
     share = h1buf[0]
     for r in range(1, nrow):
@@ -375,13 +378,17 @@
     pair = remote(pairsend, pairbuf, pair_sem.at[0], pair_sem.at[1], partner)
     pair.start()
 
-    got(-2)
+    got(half_slot(-2, 0), 0)
     copies[0].start()
     copies[1].start()
-    share_chunk(slot(-2), -2).start()
-    got(2)
+    got(half_slot(2, 1), 3)
     copies[2].start()
     copies[3].start()
+    got(half_slot(-2, 1), 1)
+    copies[4].start()
+    got(half_slot(2, 0), 2)
+    copies[5].start()
+    share_chunk(slot(-2), -2).start()
     share_chunk(slot(2), 2).start()
 
     pair.wait_recv()
@@ -391,8 +398,8 @@
     for k in range(1, nz):
         remote(h2send, h2buf.at[z], h2_ssem, h2_rsem, chip(k)).start()
 
-    for k in (1, -1):
-        got(k)
+    for k, n in ((-1, 4), (1, 5)):
+        got(slot(k), n)
         share_chunk(slot(k), k).start()
 
     own_reflectors = exact(mixing_t, headbuf[...])
@@ -405,12 +412,13 @@
 
     own_base = exact(second_t, obuf[...])
 
-    for k in (3, -3):
-        got(k)
+    got(half_slot(4, 0), 10)
+    got(half_slot(4, 1), 11)
+    share_chunk(slot(4), 4).start()
+    for k, n in ((-3, 6), (3, 8)):
+        got(half_slot(k, 0), n)
+        got(half_slot(k, 1), n + 1)
         share_chunk(slot(k), k).start()
-    got_half(0)
-    got_half(1)
-    share_chunk(slot(4), 4).start()
 
     others(h2buf, nz, h2_ssem, h2_rsem).wait_recv()
 
@@ -436,10 +444,9 @@
     remote(mine, mine, f_ssem, f_rsem, partner).wait_send()
     leaves(lambda copy: copy.wait_send())
     nears(lambda copy: copy.wait_send())
-    stage_two(lambda copy: copy.wait_send())
-    for k in (2, -2, 1, -1):
-        gather(k).wait_send()
-    for copy in copies:
+    for copy in stage_two:
+        copy.wait_send()
+    for copy in gather + copies:
         copy.wait_send()
     others(gbuf, nrow, g_ssem, g_rsem).wait_send()
     others(h1buf, nrow, h1_ssem, h1_rsem).wait_send()
@@ -530,7 +537,7 @@
             dma(()), dma(()),
             dma(()), dma((nz,)),
             dma((8,)), dma((8,)),
-            dma((8,)), dma((8,)),
+            dma((12,)), dma((12,)),
             dma(()), dma(()),
             dma(()), dma(()),
             dma(()), dma(()),

time: 44.3 us -> 44.2 us (level)
  no operation moved by 1% of the time
where the time goes in v5:
time: 44.2 us; the launch traced here: 44 us
  Pallas kernels  43.3 us (98%)
  between operations  0.67 us (2%)
    pallas_call x1, Pallas kernels, local(): pl.pallas_call(functools.partial(exchange_kernel, nrow, ncol), name='exch...  40.3 us
    pallas_call x1, Pallas kernels, local(): pl.pallas_call(functools.partial(update_kernel, groups), name='update', o...  3.03 us

profile of v5, /device:TPU:1, one launch (start us, length us, event | category | flops | bytes accessed | tf_op | source)
XLA Modules:
  0.0 44.0 jit_solution(3795277005023902039)
XLA Ops:
  0.6 0.0 copy-start.1
  0.6 0.0 copy-start
  0.6 40.3 %exchange.1 = (f32[16,32,512]{2,1,0:T(8,128)S(1)}, f32[128,128]{1,0:T(8,128)S(1)}) custom-call(f32[8192,128]{1,0:T(8,128)} %slab.3, f32[32,8192]{1,0:T(8,128)} %panel.3, f32[32,8192]{1,0:T(8,128)} %far.1), custom_call_target="tpu_custom_call" | custom-call | tf_op jit(solution)/shard_map/exchange/pallas_call | solution.py:511
  40.9 0.0 copy-done.1
  40.9 0.0 copy-done
  41.0 3.0 %update.1 = (f32[8192,128]{1,0:T(8,128)}, f32[32,8192]{1,0:T(8,128)}) custom-call(f32[8192,128]{1,0:T(8,128)S(1)} %copy-done, f32[32,8192]{1,0:T(8,128)S(1)} %copy-done.1, f32[16,32,512]{2,1,0:T(8,128)S(1)} %get-tuple-element.4.images, f32[128,128]{1,0:T(8,128)S(1)} %get-tuple-element.5.coefs), custom_call_target="tpu_custom_call" | custom-call | tf_op jit(solution)/shard_map/update/pallas_call | solution.py:552
Async XLA Ops:
  0.6 40.3 %copy-start.1 = (f32[32,8192]{1,0:T(8,128)S(1)}, f32[32,8192]{1,0:T(8,128)}, u32[]{:S(2)}) copy-start(f32[32,8192]{1,0:T(8,128)} %panel.3) | copy-start | bytes 3145732
  0.6 40.3 %copy-start = (f32[8192,128]{1,0:T(8,128)S(1)}, f32[8192,128]{1,0:T(8,128)}, u32[]{:S(2)}) copy-start(f32[8192,128]{1,0:T(8,128)} %slab.3) | copy-start | bytes 12582916

commit v6 on v5

--- a/solution.py
+++ b/solution.py
@@ -166,13 +166,16 @@
 
     head_columns = pl.ds(pl.multiple_of(col * 128, 128), 128)
 
+    @pl.when(row == 0)
+    def _():
+        for k in range(1, nrow):
+            remote(pv.at[:, head_columns], headbuf, t_ssem, t_rsem, {"row": row_peer(k)}).start()
+
     for k in range(1, nrow):
         remote(gsend, gbuf.at[row], g_ssem, g_rsem, {"row": row_peer(k)}).start()
 
     @pl.when(row == 0)
     def _():
-        for k in range(1, nrow):
-            remote(pv.at[:, head_columns], headbuf, t_ssem, t_rsem, {"row": row_peer(k)}).start()
         local_head = pltpu.make_async_copy(pv.at[:, head_columns], headbuf, load_sem.at[3])
         local_head.start()
         local_head.wait()

time: 44.2 us -> 44 us (level)
  no operation moved by 1% of the time
where the time goes in v6:
time: 44 us; the launch traced here: 43.9 us
  Pallas kernels  43.2 us (98%)
  between operations  0.67 us (2%)
    pallas_call x1, Pallas kernels, local(): pl.pallas_call(functools.partial(exchange_kernel, nrow, ncol), name='exch...  40.2 us
    pallas_call x1, Pallas kernels, local(): pl.pallas_call(functools.partial(update_kernel, groups), name='update', o...  3.04 us

profile of v6, /device:TPU:1, one launch (start us, length us, event | category | flops | bytes accessed | tf_op | source)
XLA Modules:
  0.0 43.9 jit_solution(12895397446065034810)
XLA Ops:
  0.6 0.0 copy-start.1
  0.6 0.0 copy-start
  0.6 40.2 %exchange.1 = (f32[16,32,512]{2,1,0:T(8,128)S(1)}, f32[128,128]{1,0:T(8,128)S(1)}) custom-call(f32[8192,128]{1,0:T(8,128)} %slab.3, f32[32,8192]{1,0:T(8,128)} %panel.3, f32[32,8192]{1,0:T(8,128)} %far.1), custom_call_target="tpu_custom_call" | custom-call | tf_op jit(solution)/shard_map/exchange/pallas_call | solution.py:514
  40.8 0.0 copy-done.1
  40.8 0.0 copy-done
  40.8 3.0 %update.1 = (f32[8192,128]{1,0:T(8,128)}, f32[32,8192]{1,0:T(8,128)}) custom-call(f32[8192,128]{1,0:T(8,128)S(1)} %copy-done, f32[32,8192]{1,0:T(8,128)S(1)} %copy-done.1, f32[16,32,512]{2,1,0:T(8,128)S(1)} %get-tuple-element.4.images, f32[128,128]{1,0:T(8,128)S(1)} %get-tuple-element.5.coefs), custom_call_target="tpu_custom_call" | custom-call | tf_op jit(solution)/shard_map/update/pallas_call | solution.py:555
Async XLA Ops:
  0.6 40.2 %copy-start.1 = (f32[32,8192]{1,0:T(8,128)S(1)}, f32[32,8192]{1,0:T(8,128)}, u32[]{:S(2)}) copy-start(f32[32,8192]{1,0:T(8,128)} %panel.3) | copy-start | bytes 3145732
  0.6 40.2 %copy-start = (f32[8192,128]{1,0:T(8,128)S(1)}, f32[8192,128]{1,0:T(8,128)}, u32[]{:S(2)}) copy-start(f32[8192,128]{1,0:T(8,128)} %slab.3) | copy-start | bytes 12582916

commit v7 on v6

--- a/solution.py
+++ b/solution.py
@@ -415,13 +415,13 @@
 
     own_base = exact(second_t, obuf[...])
 
-    got(half_slot(4, 0), 10)
-    got(half_slot(4, 1), 11)
-    share_chunk(slot(4), 4).start()
     for k, n in ((-3, 6), (3, 8)):
         got(half_slot(k, 0), n)
         got(half_slot(k, 1), n + 1)
         share_chunk(slot(k), k).start()
+    got(half_slot(4, 0), 10)
+    got(half_slot(4, 1), 11)
+    share_chunk(slot(4), 4).start()
 
     others(h2buf, nz, h2_ssem, h2_rsem).wait_recv()
 

time: 44 us -> 43.8 us (level)
  no operation moved by 1% of the time
where the time goes in v7:
time: 43.8 us; the launch traced here: 43.7 us
  Pallas kernels  43 us (98%)
  between operations  0.67 us (2%)
    pallas_call x1, Pallas kernels, local(): pl.pallas_call(functools.partial(exchange_kernel, nrow, ncol), name='exch...  40 us
    pallas_call x1, Pallas kernels, local(): pl.pallas_call(functools.partial(update_kernel, groups), name='update', o...  3.02 us

profile of v7, /device:TPU:1, one launch (start us, length us, event | category | flops | bytes accessed | tf_op | source)
XLA Modules:
  0.0 43.7 jit_solution(14319674502049759078)
XLA Ops:
  0.6 0.0 copy-start.1
  0.6 0.0 copy-start
  0.6 40.0 %exchange.1 = (f32[16,32,512]{2,1,0:T(8,128)S(1)}, f32[128,128]{1,0:T(8,128)S(1)}) custom-call(f32[8192,128]{1,0:T(8,128)} %slab.3, f32[32,8192]{1,0:T(8,128)} %panel.3, f32[32,8192]{1,0:T(8,128)} %far.1), custom_call_target="tpu_custom_call" | custom-call | tf_op jit(solution)/shard_map/exchange/pallas_call | solution.py:514
  40.6 0.0 copy-done.1
  40.6 0.0 copy-done
  40.7 3.0 %update.1 = (f32[8192,128]{1,0:T(8,128)}, f32[32,8192]{1,0:T(8,128)}) custom-call(f32[8192,128]{1,0:T(8,128)S(1)} %copy-done, f32[32,8192]{1,0:T(8,128)S(1)} %copy-done.1, f32[16,32,512]{2,1,0:T(8,128)S(1)} %get-tuple-element.4.images, f32[128,128]{1,0:T(8,128)S(1)} %get-tuple-element.5.coefs), custom_call_target="tpu_custom_call" | custom-call | tf_op jit(solution)/shard_map/update/pallas_call | solution.py:555
Async XLA Ops:
  0.6 40.0 %copy-start.1 = (f32[32,8192]{1,0:T(8,128)S(1)}, f32[32,8192]{1,0:T(8,128)}, u32[]{:S(2)}) copy-start(f32[32,8192]{1,0:T(8,128)} %panel.3) | copy-start | bytes 3145732
  0.6 40.0 %copy-start = (f32[8192,128]{1,0:T(8,128)S(1)}, f32[8192,128]{1,0:T(8,128)}, u32[]{:S(2)}) copy-start(f32[8192,128]{1,0:T(8,128)} %slab.3) | copy-start | bytes 12582916
